TPU v7x, 256 devices: a whole 4x4x8 slice. The times are simulated.
256 devices in a mesh: scen: 8 (over x, y_hi), rows: 32 (over z, y_lo, core).
Axes of the slice: x: 4, y: 4 (y_hi: 2, y_lo: 2; y = y_hi * 2 + y_lo), z: 8, core: 2. Of those that a mesh axis runs over, the one named last changes fastest.
Arguments:
- factor_rows: float32 [32, 16384, 1024], P('scen', 'rows'), may hold values from -1.5 to 1.5
- panel_factor: float32 [32, 1024, 512], P('scen'), may hold values from -0.03125 to 0.03125
- pivot_add: float32 [512, 512], replicated, may hold values from -1 to 4, as said below
- trailing: float32 [16384, 4096], P('rows', 'scen'), may hold values from -6 to 6
Outputs:
- panel: float32 [16384, 512], P('rows')
- updated: float32 [16384, 4096], P('rows', 'scen')
Inputs may be any that keep to these rules, and one draw needn't show every extreme that they name: `pivot_add`: symmetric positive definite; its diagonal lies between 1 and 3 and its off-diagonal entries are small.
All inputs are finite; a program needn't handle non-finite values.
Results may differ from a plain program's by a relative error of at most 0.0001.
Values sent between devices are 32-bit elements; how exact they have to be, the bound alone decides.
No kernel may reach another device: no remote copies, remote signals or barrier semaphores. Data moves between devices by JAX's collectives and lax.ppermute only.
A program may use at most 128 MiB of HBM per device.

v0:
```python
import jax
import jax.numpy as jnp
from jax import lax
from jax.experimental import pallas as pl
from jax.experimental.pallas import tpu as pltpu
from jax.sharding import PartitionSpec as P


N = 512
B = 128
EXACT = lax.Precision.HIGHEST
VMEM = pl.BlockSpec(memory_space=pltpu.VMEM)
SMEM = pl.BlockSpec(memory_space=pltpu.SMEM)


def spread(x):
    return jnp.broadcast_to(x, (8, 128))


def factor_block(sv, ev):
    sub = lax.broadcasted_iota(jnp.int32, (8, 128), 0)
    for b in range(16):
        col = {v: [spread(sv[v][:, 8 * b + i : 8 * b + i + 1]) for i in range(8)] for v in range(b, 16)}
        trow = [spread(sv[b][i : i + 1, :]) for i in range(8)]
        frow = [spread(ev[b][i : i + 1, :]) for i in range(8)]
        el = [[spread(col[b][j][i : i + 1, :]) for j in range(i + 1)] for i in range(8)]
        low = [[None] * 8 for _ in range(8)]
        inv = [None] * 8
        for j in range(8):
            inv[j] = lax.rsqrt(el[j][j])
            for i in range(j + 1, 8):
                low[i][j] = el[i][j] * inv[j]
            for i in range(j + 1, 8):
                for m in range(j + 1, i + 1):
                    el[i][m] = el[i][m] - low[i][j] * low[m][j]
            trow[j] = trow[j] * inv[j]
            frow[j] = frow[j] * inv[j]
            for i in range(j + 1, 8):
                trow[i] = trow[i] - low[i][j] * trow[j]
                frow[i] = frow[i] - low[i][j] * frow[j]
        for v in range(b + 1, 16):
            c = col[v]
            for j in range(8):
                c[j] = c[j] * inv[j]
                for i in range(j + 1, 8):
                    c[i] = c[i] - low[i][j] * c[j]
            for j in range(8):
                sv[v] = sv[v] - c[j] * trow[j]
                ev[v] = ev[v] - c[j] * frow[j]
        out = frow[0]
        for i in range(1, 8):
            out = jnp.where(sub == i, frow[i], out)
        ev[b] = out
    return ev


def dot(a, b, ca, cb):
    return lax.dot_general(a, b, (((ca,), (cb,)), ((), ())), precision=EXACT, preferred_element_type=jnp.float32)


def halves(a):
    hi = a.astype(jnp.bfloat16)
    return hi, (a - hi.astype(jnp.float32)).astype(jnp.bfloat16)


def dot3(a, b, ca, cb):
    def one(x, y):
        return lax.dot_general(x, y, (((ca,), (cb,)), ((), ())), preferred_element_type=jnp.float32)

    return one(a[0], b[0]) + (one(a[0], b[1]) + one(a[1], b[0]))


def gram_kernel(pos_ref, p_ref, out_ref, acc_ref):
    piece = pos_ref[0] & 7

    @pl.when(pl.program_id(0) == 0)
    def _():
        acc_ref[...] = jnp.zeros(acc_ref.shape, jnp.float32)

    wide = halves(p_ref[0])
    part = halves(p_ref[0, :, pl.ds(pl.multiple_of(128 * (piece >> 1), 128), 128)])
    acc_ref[...] += dot3(part, wide, 0, 0)

    @pl.when(pl.program_id(0) == pl.num_programs(0) - 1)
    def _():
        out_ref[...] = acc_ref[pl.ds(pl.multiple_of(64 * (piece & 1), 64), 64), :]


def slab_kernel(f_ref, p_ref, out_ref):
    @pl.when((pl.program_id(0) == 0) & (pl.program_id(1) == 0))
    def _():
        out_ref[...] = jnp.zeros(out_ref.shape, jnp.float32)

    out_ref[...] += dot3(halves(f_ref[0]), halves(p_ref[0]), 1, 0)


def factor_kernel(pos_ref, *refs):
    add_ref, m_ref, s_ref = refs[8:]
    for k in range(8):
        at = pl.ds(pl.multiple_of(64 * ((pos_ref[0] & 7) ^ k), 64), 64)
        s_ref[at, :] = refs[k][...] + add_ref[at, :]
    rows = lax.broadcasted_iota(jnp.int32, (8, 128), 0)
    lanes = lax.broadcasted_iota(jnp.int32, (8, 128), 1)
    m_ref[...] = jnp.zeros((N, N), jnp.float32)
    for k in range(4):
        lo = B * k
        hi = lo + B
        sv = [s_ref[lo + 8 * v : lo + 8 * v + 8, lo:hi] for v in range(16)]
        ev = [jnp.where(lanes == rows + 8 * v, 1.0, 0.0).astype(jnp.float32) for v in range(16)]
        mk = jnp.concatenate(factor_block(sv, ev), axis=0)
        if k:
            m_ref[lo:hi, :lo] = dot(mk, m_ref[lo:hi, :lo], 1, 0)
        m_ref[lo:hi, lo:hi] = mk
        if k < 3:
            p = dot(s_ref[hi:, lo:hi], mk, 1, 1)
            s_ref[hi:, hi:] = s_ref[hi:, hi:] - dot(p, p, 1, 1)
            m_ref[hi:, :hi] = m_ref[hi:, :hi] - dot(p, m_ref[lo:hi, :hi], 1, 0)


def update_kernel(pos_ref, m_ref, trail_ref, slab_ref, *refs):
    panel_ref, out_ref, x_ref = refs[4:]
    for q in range(4):
        for z in range(8):
            at = pl.ds(pl.multiple_of(16 * (4 * z + ((pos_ref[0] & 3) ^ q)), 16), 16)
            x_ref[at, :] = refs[q][16 * z : 16 * z + 16, :]
    inv = halves(m_ref[...])
    panel = dot3(halves(slab_ref[...]), inv, 1, 1)
    panel_ref[...] = panel
    cross = dot3(halves(x_ref[...]), inv, 1, 1)
    out_ref[...] = trail_ref[...] - dot3(halves(panel), halves(cross), 1, 1)


def shape(n):
    return jax.ShapeDtypeStruct((n, N), jnp.float32)


def swap(x, axis, groups=None):
    return lax.all_to_all(x, axis, split_axis=0, concat_axis=0, axis_index_groups=groups, tiled=True)


def gathered(x, axis, groups=None):
    return swap(jnp.broadcast_to(x[None], (8, *x.shape)), axis, groups).reshape(-1, N)


def flip(x, axis, bits):
    n = lax.axis_size(axis)
    return lax.ppermute(x, axis, [(i, i ^ bits) for i in range(n)])


def per_device(factor_rows, panel_factor, pivot_add, trailing):
    groups, depth, _ = panel_factor.shape
    pos = lax.axis_index("rows").astype(jnp.int32).reshape(1)
    gram = pl.pallas_call(
        gram_kernel,
        grid=(groups,),
        out_shape=shape(64),
        in_specs=[SMEM, pl.BlockSpec((1, depth, N), lambda g: (g, 0, 0))],
        out_specs=pl.BlockSpec((64, N), lambda g: (0, 0)),
        scratch_shapes=[pltpu.VMEM((128, N), jnp.float32)],
        compiler_params=pltpu.CompilerParams(vmem_limit_bytes=56 << 20),
        name="gram",
    )(pos, panel_factor)
    slab = pl.pallas_call(
        slab_kernel,
        grid=(groups, depth // 512),
        out_shape=shape(N),
        in_specs=[
            pl.BlockSpec((1, N, 512), lambda g, k: (g, 0, k)),
            pl.BlockSpec((1, 512, N), lambda g, k: (g, k, 0)),
        ],
        out_specs=pl.BlockSpec((N, N), lambda g, k: (0, 0)),
        compiler_params=pltpu.CompilerParams(vmem_limit_bytes=56 << 20),
        name="slab",
    )(factor_rows, panel_factor)

    own = swap(slab.reshape(8, 64, N), "scen")
    own = own.sum(0)
    gram = gram + flip(gram, "scen", 1)
    gram = (gram + flip(gram, "scen", 2)) + (flip(gram, "scen", 4) + flip(gram, "scen", 6))
    near = [gram]
    for b in (2, 4, 6):
        near.append(flip(gram, "rows", b))
    far = [flip(x, "rows", 1) for x in near]
    pieces = [x for pair in zip(near, far) for x in pair]
    m = pl.pallas_call(
        factor_kernel,
        out_shape=shape(N),
        in_specs=[SMEM] + [VMEM] * 9,
        out_specs=VMEM,
        scratch_shapes=[pltpu.VMEM((N, N), jnp.float32)],
        compiler_params=pltpu.CompilerParams(vmem_limit_bytes=12 << 20),
        name="factor",
    )(pos, *pieces, pivot_add)

    column = [[4 * z + k for z in range(8)] for k in range(4)]
    cross = [gathered(own[:16], "rows", column)]
    cross.append(flip(cross[0], "rows", 1))
    cross += [flip(cross[0], "rows", 2)]
    cross.append(flip(cross[2], "rows", 1))
    whole = gathered(own, "scen")
    return pl.pallas_call(
        update_kernel,
        out_shape=(shape(N), shape(N)),
        in_specs=[SMEM] + [VMEM] * 7,
        out_specs=(VMEM, VMEM),
        scratch_shapes=[pltpu.VMEM((N, N), jnp.float32)],
        compiler_params=pltpu.CompilerParams(vmem_limit_bytes=28 << 20),
        name="update",
    )(pos, m, trailing, whole, *cross)


def solution(mesh):
    return jax.shard_map(
        per_device,
        mesh=mesh,
        in_specs=(P("scen", "rows", None), P("scen", None, None), P(), P("rows", "scen")),
        out_specs=(P("rows", None), P("rows", "scen")),
        check_vma=False,
    )
```

profile of v0, /device:TPU:1, one launch (start us, length us, event | category | flops | bytes accessed | tf_op | source)
XLA Modules:
  0.0 126.0 jit_solution(8438453524179940116)
XLA Ops:
  0.6 12.6 %slab.1 = f32[512,512]{1,0:T(8,128)} custom-call(f32[4,512,1024]{2,1,0:T(8,128)} %f_ref.1, f32[4,1024,512]{2,1,0:T(8,128)} %p_ref.3), custom_call_target="tpu_custom_call" | custom-call | tf_op jit(solution)/shard_map/slab/pallas_call | solution.py:163
  13.2 22.8 %all_to_all.15 = f32[8,64,512]{2,1,0:T(8,128)S(1)} all-to-all(f32[8,64,512]{2,1,0:T(8,128)} %bitcast.8), channel_id=1, replica_groups=mesh['scen'=8,'rows'=32] {'scen'}, dimensions={0} | all-to-all | bytes 2097152 | tf_op jit(solution)/shard_map/all_to_all | solution.py:138
  36.0 0.1 reduce_sum.9
  36.1 0.0 copy-start
  36.1 17.5 %all_to_all.16 = f32[8,16,512]{2,1,0:T(8,128)S(1)} all-to-all(f32[8,16,512]{2,1,0:T(8,128)S(1)} %broadcast_in_dim.5), channel_id=1, replica_groups={{0,4,8,12,16,20,24,28},{1,5,9,13,17,21,25,29},{2,6,10,14,18,22,26,30},{..., dimensions={0} | all-to-all | bytes 524288 | tf_op jit(solution)/shard_map/all_to_all | solution.py:138
  53.6 1.1 broadcast_in_dim.4
  54.7 3.6 %all-to-all-start.1 = ((f32[8,64,512]{2,1,0:T(8,128)}), f32[8,64,512]{2,1,0:T(8,128)S(1)}, u32[]{:S(2)}, u32[]{:S(2)}) async-start(f32[8,64,512]{2,1,0:T(8,128)} %broadcast_in_dim.4), calls=%async_computation.1 | async-start | bytes 2097152 | tf_op jit(solution)/shard_map/all_to_all | solution.py:138
  58.3 6.1 %gram.1 = f32[64,512]{1,0:T(8,128)} custom-call(s32[1]{0:T(128)} %bitcast.pos_ref, f32[4,1024,512]{2,1,0:T(8,128)} %p_ref.3), custom_call_target="tpu_custom_call" | custom-call | tf_op jit(solution)/shard_map/gram/pallas_call | solution.py:153
  64.4 2.8 %collective-permute-start = (f32[64,512]{1,0:T(8,128)}, f32[64,512]{1,0:T(8,128)S(1)}, u32[]{:S(2)}, u32[]{:S(2)}) collective-permute-start(f32[64,512]{1,0:T(8,128)} %gram.1), channel_id=1, source_target_pairs={{0,32},{32,0},{64,96},{96,64},{128,160},{160,128},{192,224},{224,1... | collective-permute-start | bytes 393224 | tf_op jit(solution)/shard_map/ppermute | solution.py:147
  67.3 9.2 %collective-permute-done = f32[64,512]{1,0:T(8,128)S(1)} collective-permute-done((f32[64,512]{1,0:T(8,128)}, f32[64,512]{1,0:T(8,128)S(1)}, u32[]{:S(2)}, u32[]{:S(2)}) %collective-permute-start) | collective-permute-done | bytes 131104 | tf_op jit(solution)/shard_map/ppermute | solution.py:147
  76.5 0.9 add.12
  77.4 1.5 %collective-permute-start.3 = (f32[64,512]{1,0:T(8,128)S(1)}, f32[64,512]{1,0:T(8,128)S(1)}, u32[]{:S(2)}, u32[]{:S(2)}) collective-permute-start(f32[64,512]{1,0:T(8,128)S(1)} %add.12), channel_id=1, source_target_pairs={{0,192},{32,224},{64,128},{96,160},{128,64},{160,96},{192,0},{224,... | collective-permute-start | bytes 393224 | tf_op jit(solution)/shard_map/ppermute | solution.py:147
  78.9 0.9 collective-permute-start.2
  79.8 0.9 collective-permute-start.1
  80.8 0.4 collective-permute-start.12
  81.2 1.4 %collective-permute-done.3 = f32[64,512]{1,0:T(8,128)S(1)} collective-permute-done((f32[64,512]{1,0:T(8,128)S(1)}, f32[64,512]{1,0:T(8,128)S(1)}, u32[]{:S(2)}, u32[]{:S(2)}) %collective-permute-start.3) | collective-permute-done | bytes 131104 | tf_op jit(solution)/shard_map/ppermute | solution.py:147
  82.5 1.8 %collective-permute-done.2 = f32[64,512]{1,0:T(8,128)S(1)} collective-permute-done((f32[64,512]{1,0:T(8,128)S(1)}, f32[64,512]{1,0:T(8,128)S(1)}, u32[]{:S(2)}, u32[]{:S(2)}) %collective-permute-start.2) | collective-permute-done | bytes 131104 | tf_op jit(solution)/shard_map/ppermute | solution.py:147
  84.3 0.8 collective-permute-done.1
  85.2 0.4 collective-permute-start.9
  85.6 1.2 collective-permute-start.7
  86.9 1.1 collective-permute-start.5
  87.9 3.7 %collective-permute-start.4 = (f32[64,512]{1,0:T(8,128)S(1)}, f32[64,512]{1,0:T(8,128)S(1)}, u32[]{:S(2)}, u32[]{:S(2)}) collective-permute-start(f32[64,512]{1,0:T(8,128)S(1)} %add_add_fusion.refs_0_), channel_id=1, source_target_pairs={{0,1},{1,0},{2,3},{3,2},{4,5},{5,4},{6,7},{7,6},{8,9},{9,8},{10,11... | collective-permute-start | bytes 393224 | tf_op jit(solution)/shard_map/ppermute | solution.py:147
  91.6 0.0 collective-permute-done.9.refs_6_
  91.6 2.4 %collective-permute-start.11 = (f32[128,512]{1,0:T(8,128)S(1)}, f32[128,512]{1,0:T(8,128)S(1)}, u32[]{:S(2)}, u32[]{:S(2)}) collective-permute-start(f32[128,512]{1,0:T(8,128)S(1)} %bitcast.6), channel_id=1, source_target_pairs={{0,1},{1,0},{2,3},{3,2},{4,5},{5,4},{6,7},{7,6},{8,9},{9,8},{10,11... | collective-permute-start | bytes 786440 | tf_op jit(solution)/shard_map/ppermute | solution.py:147
  94.0 0.0 collective-permute-done.12.refs_2_
  94.0 0.0 collective-permute-start.13
  94.0 0.0 collective-permute-done.7.refs_4_
  94.0 0.6 collective-permute-start.10
  94.6 0.0 collective-permute-done.5.refs_2_
  94.6 0.8 collective-permute-start.8
  95.4 0.0 collective-permute-done.4.refs_1_
  95.4 0.0 collective-permute-start.6
  95.4 0.5 collective-permute-done.10.refs_7_
  96.0 0.4 collective-permute-done.8.refs_5_
  96.4 0.4 collective-permute-done.6.refs_3_
  96.8 0.0 copy-start.1
  96.8 1.2 copy-done.1
  98.0 21.5 %factor.1.m_ref = f32[512,512]{1,0:T(8,128)S(1)} custom-call(s32[1]{0:T(128)} %bitcast.pos_ref, f32[64,512]{1,0:T(8,128)S(1)} %add_add_fusion.refs_0_, f32[64,512]{1,0:T(8,128)S(1)} %collective-permute-done.4.refs_1_, f32[64,512]{1,0:T(8,128)S(1)} %collective-permute-done.5.refs_2_, f32[64,512]{1,0:T(8,128)S(1)} %collective-permute-done.6.refs_3_, ...), custom_call_target="tpu_custom_call" | custom-call | tf_op jit(solution)/shard_map/factor/pallas_call | solution.py:185
  119.5 0.0 collective-permute-done.11.refs_1_
  119.5 0.0 copy-start.2
  119.6 0.7 copy-done.2
  120.2 0.0 all-to-all-done.1
  120.3 0.0 collective-permute-done.13.refs_3_
  120.3 0.0 copy-done
  120.3 0.0 copy-start.3
  120.3 0.9 copy-done.3
  121.2 4.8 %update.1 = (f32[512,512]{1,0:T(8,128)}, f32[512,512]{1,0:T(8,128)}) custom-call(s32[1]{0:T(128)} %bitcast.pos_ref, f32[512,512]{1,0:T(8,128)S(1)} %factor.1.m_ref, f32[512,512]{1,0:T(8,128)S(1)} %copy-done, f32[512,512]{1,0:T(8,128)S(1)} %bitcast.4, f32[128,512]{1,0:T(8,128)S(1)} %bitcast.7, f32[128,512]{1,0:T(8,128)S(1)} %copy-done.3, ...), custom_call_target="tpu_custom_call" | custom-call | tf_op jit(solution)/shard_map/update/pallas_call | solution.py:201
  (3 shorter events, 0.1 us)
Async XLA Ops:
  36.1 84.2 %copy-start = (f32[512,512]{1,0:T(8,128)S(1)}, f32[512,512]{1,0:T(8,128)}, u32[]{:S(2)}) copy-start(f32[512,512]{1,0:T(8,128)} %trail_ref.1) | copy-start | bytes 3145732
  54.7 65.5 %all-to-all-start.1 = ((f32[8,64,512]{2,1,0:T(8,128)}), f32[8,64,512]{2,1,0:T(8,128)S(1)}, u32[]{:S(2)}, u32[]{:S(2)}) async-start(f32[8,64,512]{2,1,0:T(8,128)} %broadcast_in_dim.4), calls=%async_computation.1 | async-start | bytes 2097152 | tf_op jit(solution)/shard_map/all_to_all | solution.py:138
  64.4 12.0 %collective-permute-start = (f32[64,512]{1,0:T(8,128)}, f32[64,512]{1,0:T(8,128)S(1)}, u32[]{:S(2)}, u32[]{:S(2)}) collective-permute-start(f32[64,512]{1,0:T(8,128)} %gram.1), channel_id=1, source_target_pairs={{0,32},{32,0},{64,96},{96,64},{128,160},{160,128},{192,224},{224,1... | collective-permute-start | bytes 393224 | tf_op jit(solution)/shard_map/ppermute | solution.py:147
  77.4 5.1 %collective-permute-start.3 = (f32[64,512]{1,0:T(8,128)S(1)}, f32[64,512]{1,0:T(8,128)S(1)}, u32[]{:S(2)}, u32[]{:S(2)}) collective-permute-start(f32[64,512]{1,0:T(8,128)S(1)} %add.12), channel_id=1, source_target_pairs={{0,192},{32,224},{64,128},{96,160},{128,64},{160,96},{192,0},{224,... | collective-permute-start | bytes 393224 | tf_op jit(solution)/shard_map/ppermute | solution.py:147
  78.9 5.4 %collective-permute-start.2 = (f32[64,512]{1,0:T(8,128)S(1)}, f32[64,512]{1,0:T(8,128)S(1)}, u32[]{:S(2)}, u32[]{:S(2)}) collective-permute-start(f32[64,512]{1,0:T(8,128)S(1)} %add.12), channel_id=1, source_target_pairs={{0,128},{32,160},{64,192},{96,224},{128,0},{160,32},{192,64},{224,... | collective-permute-start | bytes 393224 | tf_op jit(solution)/shard_map/ppermute | solution.py:147
  79.8 5.4 %collective-permute-start.1 = (f32[64,512]{1,0:T(8,128)S(1)}, f32[64,512]{1,0:T(8,128)S(1)}, u32[]{:S(2)}, u32[]{:S(2)}) collective-permute-start(f32[64,512]{1,0:T(8,128)S(1)} %add.12), channel_id=1, source_target_pairs={{0,64},{32,96},{64,0},{96,32},{128,192},{160,224},{192,128},{224,1... | collective-permute-start | bytes 393224 | tf_op jit(solution)/shard_map/ppermute | solution.py:147
  80.8 13.3 %collective-permute-start.12 = (f32[128,512]{1,0:T(8,128)S(1)}, f32[128,512]{1,0:T(8,128)}, u32[]{:S(2)}, u32[]{:S(2)}) collective-permute-start(f32[128,512]{1,0:T(8,128)S(1)} %bitcast.5), channel_id=1, source_target_pairs={{0,2},{1,3},{2,0},{3,1},{4,6},{5,7},{6,4},{7,5},{8,10},{9,11},{10,... | collective-permute-start | bytes 786440 | tf_op jit(solution)/shard_map/ppermute | solution.py:147
  85.2 6.4 %collective-permute-start.9 = (f32[64,512]{1,0:T(8,128)S(1)}, f32[64,512]{1,0:T(8,128)S(1)}, u32[]{:S(2)}, u32[]{:S(2)}) collective-permute-start(f32[64,512]{1,0:T(8,128)S(1)} %add_add_fusion.refs_0_), channel_id=1, source_target_pairs={{0,6},{1,7},{2,4},{3,5},{4,2},{5,3},{6,0},{7,1},{8,14},{9,15},{10,... | collective-permute-start | bytes 393224 | tf_op jit(solution)/shard_map/ppermute | solution.py:147
  85.6 8.4 %collective-permute-start.7 = (f32[64,512]{1,0:T(8,128)S(1)}, f32[64,512]{1,0:T(8,128)S(1)}, u32[]{:S(2)}, u32[]{:S(2)}) collective-permute-start(f32[64,512]{1,0:T(8,128)S(1)} %add_add_fusion.refs_0_), channel_id=1, source_target_pairs={{0,4},{1,5},{2,6},{3,7},{4,0},{5,1},{6,2},{7,3},{8,12},{9,13},{10,... | collective-permute-start | bytes 393224 | tf_op jit(solution)/shard_map/ppermute | solution.py:147
  86.9 7.8 %collective-permute-start.5 = (f32[64,512]{1,0:T(8,128)S(1)}, f32[64,512]{1,0:T(8,128)S(1)}, u32[]{:S(2)}, u32[]{:S(2)}) collective-permute-start(f32[64,512]{1,0:T(8,128)S(1)} %add_add_fusion.refs_0_), channel_id=1, source_target_pairs={{0,2},{1,3},{2,0},{3,1},{4,6},{5,7},{6,4},{7,5},{8,10},{9,11},{10,... | collective-permute-start | bytes 393224 | tf_op jit(solution)/shard_map/ppermute | solution.py:147
  87.9 7.5 %collective-permute-start.4 = (f32[64,512]{1,0:T(8,128)S(1)}, f32[64,512]{1,0:T(8,128)S(1)}, u32[]{:S(2)}, u32[]{:S(2)}) collective-permute-start(f32[64,512]{1,0:T(8,128)S(1)} %add_add_fusion.refs_0_), channel_id=1, source_target_pairs={{0,1},{1,0},{2,3},{3,2},{4,5},{5,4},{6,7},{7,6},{8,9},{9,8},{10,11... | collective-permute-start | bytes 393224 | tf_op jit(solution)/shard_map/ppermute | solution.py:147
  91.6 27.9 %collective-permute-start.11 = (f32[128,512]{1,0:T(8,128)S(1)}, f32[128,512]{1,0:T(8,128)S(1)}, u32[]{:S(2)}, u32[]{:S(2)}) collective-permute-start(f32[128,512]{1,0:T(8,128)S(1)} %bitcast.6), channel_id=1, source_target_pairs={{0,1},{1,0},{2,3},{3,2},{4,5},{5,4},{6,7},{7,6},{8,9},{9,8},{10,11... | collective-permute-start | bytes 786440 | tf_op jit(solution)/shard_map/ppermute | solution.py:147
  94.0 26.2 %collective-permute-start.13 = (f32[128,512]{1,0:T(8,128)}, f32[128,512]{1,0:T(8,128)}, u32[]{:S(2)}, u32[]{:S(2)}) collective-permute-start(f32[128,512]{1,0:T(8,128)} %collective-permute-done.12.refs_2_), channel_id=1, source_target_pairs={{0,1},{1,0},{2,3},{3,2},{4,5},{5,4},{6,7},{7,6},{8,9},{9,8},{10,11... | collective-permute-start | bytes 786440 | tf_op jit(solution)/shard_map/ppermute | solution.py:147
  94.0 1.9 %collective-permute-start.10 = (f32[64,512]{1,0:T(8,128)S(1)}, f32[64,512]{1,0:T(8,128)S(1)}, u32[]{:S(2)}, u32[]{:S(2)}) collective-permute-start(f32[64,512]{1,0:T(8,128)S(1)} %collective-permute-done.9.refs_6_), channel_id=1, source_target_pairs={{0,1},{1,0},{2,3},{3,2},{4,5},{5,4},{6,7},{7,6},{8,9},{9,8},{10,11... | collective-permute-start | bytes 393224 | tf_op jit(solution)/shard_map/ppermute | solution.py:147
  94.6 1.8 %collective-permute-start.8 = (f32[64,512]{1,0:T(8,128)S(1)}, f32[64,512]{1,0:T(8,128)S(1)}, u32[]{:S(2)}, u32[]{:S(2)}) collective-permute-start(f32[64,512]{1,0:T(8,128)S(1)} %collective-permute-done.7.refs_4_), channel_id=1, source_target_pairs={{0,1},{1,0},{2,3},{3,2},{4,5},{5,4},{6,7},{7,6},{8,9},{9,8},{10,11... | collective-permute-start | bytes 393224 | tf_op jit(solution)/shard_map/ppermute | solution.py:147
  95.4 1.3 %collective-permute-start.6 = (f32[64,512]{1,0:T(8,128)S(1)}, f32[64,512]{1,0:T(8,128)S(1)}, u32[]{:S(2)}, u32[]{:S(2)}) collective-permute-start(f32[64,512]{1,0:T(8,128)S(1)} %collective-permute-done.5.refs_2_), channel_id=1, source_target_pairs={{0,1},{1,0},{2,3},{3,2},{4,5},{5,4},{6,7},{7,6},{8,9},{9,8},{10,11... | collective-permute-start | bytes 393224 | tf_op jit(solution)/shard_map/ppermute | solution.py:147
  96.8 1.2 copy-start.1
  119.5 0.7 copy-start.2
  120.3 1.0 copy-start.3
where the time goes:
time: 127 us; the launch traced here: 126 us
  Pallas kernels  45 us (35%)
  blocking collectives  40.3 us (32%)
  starting transfers between devices  20.3 us (16%)
  waiting for transfers between devices  14.6 us (11%)
  local copies, waits for them, and re-layouts  3.99 us (3%)
    all_to_all x2, blocking collectives, swap(): lax.all_to_all(x, axis, split_axis=0, concat_axis=0, axis_index_groups=gr...  40.3 us
    pallas_call x1, Pallas kernels, per_device(): pl.pallas_call(factor_kernel, out_shape=shape(N), in_specs=[SMEM] + [VMEM...  21.5 us
    ppermute x14, starting transfers between devices, flip(): return lax.ppermute(x, axis, [(i, i ^ bits) for i in range(n)])  16.8 us
    ppermute x14, waiting for transfers between devices, flip(): return lax.ppermute(x, axis, [(i, i ^ bits) for i in range(n)])  14.6 us
    pallas_call x1, Pallas kernels, per_device(): pl.pallas_call(slab_kernel, grid=(groups, depth // 512), out_shape=shape(...  12.6 us
    pallas_call x1, Pallas kernels, per_device(): pl.pallas_call(gram_kernel, grid=(groups,), out_shape=shape(64), in_specs...  6.13 us
    pallas_call x1, Pallas kernels, per_device(): pl.pallas_call(update_kernel, out_shape=(shape(N), shape(N)), in_specs=[S...  4.8 us
    all_to_all x1, starting transfers between devices, swap(): lax.all_to_all(x, axis, split_axis=0, concat_axis=0, axis_index_groups=gr...  3.56 us
  transfers between devices with their start and end apart: 15, of which 7 were waited for; matrix products, arithmetic and copies ran while one was open for 1% of the time, Pallas kernels for 22%

commit v1 on v0

--- a/solution.py
+++ b/solution.py
@@ -10,6 +10,7 @@
 B = 128
 EXACT = lax.Precision.HIGHEST
 VMEM = pl.BlockSpec(memory_space=pltpu.VMEM)
+HBM = pl.BlockSpec(memory_space=pltpu.HBM)
 SMEM = pl.BlockSpec(memory_space=pltpu.SMEM)
 
 
@@ -70,35 +71,33 @@
     return one(a[0], b[0]) + (one(a[0], b[1]) + one(a[1], b[0]))
 
 
-def gram_kernel(pos_ref, p_ref, out_ref, acc_ref):
+def product_kernel(pos_ref, f_ref, p_ref, slab_ref, gram_ref, acc_ref):
     piece = pos_ref[0] & 7
 
     @pl.when(pl.program_id(0) == 0)
     def _():
         acc_ref[...] = jnp.zeros(acc_ref.shape, jnp.float32)
 
-    wide = halves(p_ref[0])
-    part = halves(p_ref[0, :, pl.ds(pl.multiple_of(128 * (piece >> 1), 128), 128)])
-    acc_ref[...] += dot3(part, wide, 0, 0)
+    part = p_ref[0, :, pl.ds(pl.multiple_of(128 * (piece >> 1), 128), 128)].T
+    acc_ref[...] += dot3(halves(jnp.concatenate([f_ref[0], part], axis=0)), halves(p_ref[0]), 1, 0)
 
     @pl.when(pl.program_id(0) == pl.num_programs(0) - 1)
     def _():
-        out_ref[...] = acc_ref[pl.ds(pl.multiple_of(64 * (piece & 1), 64), 64), :]
-
-
-def slab_kernel(f_ref, p_ref, out_ref):
-    @pl.when((pl.program_id(0) == 0) & (pl.program_id(1) == 0))
-    def _():
-        out_ref[...] = jnp.zeros(out_ref.shape, jnp.float32)
-
-    out_ref[...] += dot3(halves(f_ref[0]), halves(p_ref[0]), 1, 0)
+        slab_ref[...] = acc_ref[:N]
+        gram_ref[...] = acc_ref[pl.ds(pl.multiple_of(N + 64 * (piece & 1), 64), 64), :]
 
 
 def factor_kernel(pos_ref, *refs):
-    add_ref, m_ref, s_ref = refs[8:]
+    add_hbm, m_ref, s_ref, add_ref, sems = refs[8:]
+    copies = [pltpu.make_async_copy(add_hbm, add_ref, sems.at[8])]
     for k in range(8):
         at = pl.ds(pl.multiple_of(64 * ((pos_ref[0] & 7) ^ k), 64), 64)
-        s_ref[at, :] = refs[k][...] + add_ref[at, :]
+        copies.append(pltpu.make_async_copy(refs[k], s_ref.at[at, :], sems.at[k]))
+    for copy in copies:
+        copy.start()
+    for copy in copies:
+        copy.wait()
+    s_ref[...] = s_ref[...] + add_ref[...]
     rows = lax.broadcasted_iota(jnp.int32, (8, 128), 0)
     lanes = lax.broadcasted_iota(jnp.int32, (8, 128), 1)
     m_ref[...] = jnp.zeros((N, N), jnp.float32)
@@ -117,16 +116,20 @@
             m_ref[hi:, :hi] = m_ref[hi:, :hi] - dot(p, m_ref[lo:hi, :hi], 1, 0)
 
 
-def update_kernel(pos_ref, m_ref, trail_ref, slab_ref, *refs):
-    panel_ref, out_ref, x_ref = refs[4:]
+def update_kernel(pos_ref, m_hbm, trail_hbm, slab_hbm, *refs):
+    panel_ref, out_ref, m_ref, slab_ref, x_ref, trail_ref, sems = refs[4:]
+    copies = [pltpu.make_async_copy(slab_hbm, slab_ref, sems.at[4]), pltpu.make_async_copy(m_hbm, m_ref, sems.at[6])]
     for q in range(4):
-        for z in range(8):
-            at = pl.ds(pl.multiple_of(16 * (4 * z + ((pos_ref[0] & 3) ^ q)), 16), 16)
-            x_ref[at, :] = refs[q][16 * z : 16 * z + 16, :]
+        copies.append(pltpu.make_async_copy(refs[q], x_ref.at[:, (pos_ref[0] & 3) ^ q], sems.at[q]))
+    copies.append(pltpu.make_async_copy(trail_hbm, trail_ref, sems.at[5]))
+    for copy in copies:
+        copy.start()
+    for copy in copies:
+        copy.wait()
     inv = halves(m_ref[...])
     panel = dot3(halves(slab_ref[...]), inv, 1, 1)
     panel_ref[...] = panel
-    cross = dot3(halves(x_ref[...]), inv, 1, 1)
+    cross = dot3(halves(x_ref[...].reshape(N, N)), inv, 1, 1)
     out_ref[...] = trail_ref[...] - dot3(halves(panel), halves(cross), 1, 1)
 
 
@@ -150,28 +153,20 @@
 def per_device(factor_rows, panel_factor, pivot_add, trailing):
     groups, depth, _ = panel_factor.shape
     pos = lax.axis_index("rows").astype(jnp.int32).reshape(1)
-    gram = pl.pallas_call(
-        gram_kernel,
+    slab, gram = pl.pallas_call(
+        product_kernel,
         grid=(groups,),
-        out_shape=shape(64),
-        in_specs=[SMEM, pl.BlockSpec((1, depth, N), lambda g: (g, 0, 0))],
-        out_specs=pl.BlockSpec((64, N), lambda g: (0, 0)),
-        scratch_shapes=[pltpu.VMEM((128, N), jnp.float32)],
+        out_shape=(shape(N), shape(64)),
+        in_specs=[
+            SMEM,
+            pl.BlockSpec((1, N, depth), lambda g: (g, 0, 0)),
+            pl.BlockSpec((1, depth, N), lambda g: (g, 0, 0)),
+        ],
+        out_specs=(pl.BlockSpec((N, N), lambda g: (0, 0)), pl.BlockSpec((64, N), lambda g: (0, 0))),
+        scratch_shapes=[pltpu.VMEM((N + 128, N), jnp.float32)],
         compiler_params=pltpu.CompilerParams(vmem_limit_bytes=56 << 20),
-        name="gram",
-    )(pos, panel_factor)
-    slab = pl.pallas_call(
-        slab_kernel,
-        grid=(groups, depth // 512),
-        out_shape=shape(N),
-        in_specs=[
-            pl.BlockSpec((1, N, 512), lambda g, k: (g, 0, k)),
-            pl.BlockSpec((1, 512, N), lambda g, k: (g, k, 0)),
-        ],
-        out_specs=pl.BlockSpec((N, N), lambda g, k: (0, 0)),
-        compiler_params=pltpu.CompilerParams(vmem_limit_bytes=56 << 20),
-        name="slab",
-    )(factor_rows, panel_factor)
+        name="product",
+    )(pos, factor_rows, panel_factor)
 
     own = swap(slab.reshape(8, 64, N), "scen")
     own = own.sum(0)
@@ -185,28 +180,31 @@
     m = pl.pallas_call(
         factor_kernel,
         out_shape=shape(N),
-        in_specs=[SMEM] + [VMEM] * 9,
+        in_specs=[SMEM] + [HBM] * 9,
         out_specs=VMEM,
-        scratch_shapes=[pltpu.VMEM((N, N), jnp.float32)],
-        compiler_params=pltpu.CompilerParams(vmem_limit_bytes=12 << 20),
+        scratch_shapes=[pltpu.VMEM((N, N), jnp.float32)] * 2 + [pltpu.SemaphoreType.DMA((9,))],
         name="factor",
     )(pos, *pieces, pivot_add)
 
     column = [[4 * z + k for z in range(8)] for k in range(4)]
     cross = [gathered(own[:16], "rows", column)]
-    cross.append(flip(cross[0], "rows", 1))
-    cross += [flip(cross[0], "rows", 2)]
-    cross.append(flip(cross[2], "rows", 1))
+    cross += [flip(cross[0], "rows", q) for q in (1, 2, 3)]
     whole = gathered(own, "scen")
     return pl.pallas_call(
         update_kernel,
         out_shape=(shape(N), shape(N)),
-        in_specs=[SMEM] + [VMEM] * 7,
+        in_specs=[SMEM] + [HBM] * 7,
         out_specs=(VMEM, VMEM),
-        scratch_shapes=[pltpu.VMEM((N, N), jnp.float32)],
+        scratch_shapes=[
+            pltpu.VMEM((N, N), jnp.float32),
+            pltpu.VMEM((N, N), jnp.float32),
+            pltpu.VMEM((8, 4, 16, N), jnp.float32),
+            pltpu.VMEM((N, N), jnp.float32),
+            pltpu.SemaphoreType.DMA((7,)),
+        ],
         compiler_params=pltpu.CompilerParams(vmem_limit_bytes=28 << 20),
         name="update",
-    )(pos, m, trailing, whole, *cross)
+    )(pos, m, trailing, whole, *[x.reshape(8, 16, N) for x in cross])
 
 
 def solution(mesh):

time: 127 us -> 127 us (level)
  starting transfers between devices: 20.3 us -> 26.4 us
  Pallas kernels: 45 us -> 40.2 us
    ppermute x14, starting transfers between devices: 16.8 us -> 22.9 us  [flip(): return lax.ppermute(x, axis, [(i, i ^ bits) for i in range(n)])]
    pallas_call x3 -> x2, Pallas kernels: 40.2 us -> 36.1 us  [the longest x1 23.9 us: per_device(): pl.pallas_call(factor_kernel, out_shape=shape(N), in_specs=[SMEM] + [HBM]...]
    unnamed x8 -> x18, local copies, waits for them, and re-layouts: 2.87 us -> 1.88 us
  transfers between devices with their start and end apart: 15 -> 15, of which waited for: 7 -> 4; matrix products, arithmetic and copies ran while one was open for 1% -> 1% of each run, Pallas kernels for 22% -> 19%
where the time goes in v1:
time: 127 us
  blocking collectives  40.3 us (32%)
  Pallas kernels  40.2 us (32%)
  starting transfers between devices  26.4 us (21%)
  waiting for transfers between devices  15 us (12%)
  local copies, waits for them, and re-layouts  3.01 us (2%)
    all_to_all x2, blocking collectives, swap(): lax.all_to_all(x, axis, split_axis=0, concat_axis=0, axis_index_groups=gr...  40.3 us
    pallas_call x1, Pallas kernels, per_device(): pl.pallas_call(factor_kernel, out_shape=shape(N), in_specs=[SMEM] + [HBM]...  23.9 us
    ppermute x14, starting transfers between devices, flip(): return lax.ppermute(x, axis, [(i, i ^ bits) for i in range(n)])  22.9 us
    ppermute x14, waiting for transfers between devices, flip(): return lax.ppermute(x, axis, [(i, i ^ bits) for i in range(n)])  15 us
    pallas_call x1, Pallas kernels, per_device(): pl.pallas_call(product_kernel, grid=(groups,), out_shape=(shape(N), shape...  12.3 us
    pallas_call x1, Pallas kernels, per_device(): pl.pallas_call(update_kernel, out_shape=(shape(N), shape(N)), in_specs=[S...  4.1 us
    all_to_all x1, starting transfers between devices, swap(): lax.all_to_all(x, axis, split_axis=0, concat_axis=0, axis_index_groups=gr...  3.56 us
  transfers between devices with their start and end apart: 15, of which 4 were waited for; matrix products, arithmetic and copies ran while one was open for 1% of the time, Pallas kernels for 19%

profile of v1, /device:TPU:1, one launch (start us, length us, event | category | flops | bytes accessed | tf_op | source)
XLA Modules:
  0.0 126.9 jit_solution(17876745088140764180)
XLA Ops:
  0.6 12.3 %product.1 = (f32[512,512]{1,0:T(8,128)}, f32[64,512]{1,0:T(8,128)}) custom-call(s32[1]{0:T(128)} %bitcast.pos_ref, f32[4,512,1024]{2,1,0:T(8,128)} %f_ref.1, f32[4,1024,512]{2,1,0:T(8,128)} %p_ref.1), custom_call_target="tpu_custom_call" | custom-call | tf_op jit(solution)/shard_map/product/pallas_call | solution.py:156
  12.9 23.0 %all_to_all.15 = f32[8,64,512]{2,1,0:T(8,128)S(1)} all-to-all(f32[8,64,512]{2,1,0:T(8,128)} %bitcast.14), channel_id=1, replica_groups=mesh['scen'=8,'rows'=32] {'scen'}, dimensions={0} | all-to-all | bytes 2097152 | tf_op jit(solution)/shard_map/all_to_all | solution.py:141
  35.8 0.1 reduce_sum.9
  36.0 17.4 %all_to_all.16.refs_0_ = f32[8,16,512]{2,1,0:T(8,128)S(1)} all-to-all(f32[8,16,512]{2,1,0:T(8,128)S(1)} %broadcast_in_dim.5), channel_id=1, replica_groups={{0,4,8,12,16,20,24,28},{1,5,9,13,17,21,25,29},{2,6,10,14,18,22,26,30},{..., dimensions={0} | all-to-all | bytes 524288 | tf_op jit(solution)/shard_map/all_to_all | solution.py:141
  53.3 1.1 broadcast_in_dim.4
  54.4 3.6 %all-to-all-start.1 = ((f32[8,64,512]{2,1,0:T(8,128)}), f32[8,64,512]{2,1,0:T(8,128)S(1)}, u32[]{:S(2)}, u32[]{:S(2)}) async-start(f32[8,64,512]{2,1,0:T(8,128)} %broadcast_in_dim.4), calls=%async_computation.1 | async-start | bytes 2097152 | tf_op jit(solution)/shard_map/all_to_all | solution.py:141
  58.0 2.9 %collective-permute-start = (f32[64,512]{1,0:T(8,128)}, f32[64,512]{1,0:T(8,128)S(1)}, u32[]{:S(2)}, u32[]{:S(2)}) collective-permute-start(f32[64,512]{1,0:T(8,128)} %get-tuple-element.4), channel_id=1, source_target_pairs={{0,32},{32,0},{64,96},{96,64},{128,160},{160,128},{192,224},{224,1... | collective-permute-start | bytes 393224 | tf_op jit(solution)/shard_map/ppermute | solution.py:150
  60.9 9.4 %collective-permute-done = f32[64,512]{1,0:T(8,128)S(1)} collective-permute-done((f32[64,512]{1,0:T(8,128)}, f32[64,512]{1,0:T(8,128)S(1)}, u32[]{:S(2)}, u32[]{:S(2)}) %collective-permute-start) | collective-permute-done | bytes 131104 | tf_op jit(solution)/shard_map/ppermute | solution.py:150
  70.3 0.9 add.12
  71.2 7.3 %collective-permute-start.3 = (f32[64,512]{1,0:T(8,128)S(1)}, f32[64,512]{1,0:T(8,128)S(1)}, u32[]{:S(2)}, u32[]{:S(2)}) collective-permute-start(f32[64,512]{1,0:T(8,128)S(1)} %add.12), channel_id=1, source_target_pairs={{0,192},{32,224},{64,128},{96,160},{128,64},{160,96},{192,0},{224,... | collective-permute-start | bytes 393224 | tf_op jit(solution)/shard_map/ppermute | solution.py:150
  78.5 0.3 collective-permute-start.2
  78.7 0.4 collective-permute-start.1
  79.1 3.1 %collective-permute-done.3 = f32[64,512]{1,0:T(8,128)S(1)} collective-permute-done((f32[64,512]{1,0:T(8,128)S(1)}, f32[64,512]{1,0:T(8,128)S(1)}, u32[]{:S(2)}, u32[]{:S(2)}) %collective-permute-start.3) | collective-permute-done | bytes 131104 | tf_op jit(solution)/shard_map/ppermute | solution.py:150
  82.2 1.7 %collective-permute-done.2 = f32[64,512]{1,0:T(8,128)S(1)} collective-permute-done((f32[64,512]{1,0:T(8,128)S(1)}, f32[64,512]{1,0:T(8,128)S(1)}, u32[]{:S(2)}, u32[]{:S(2)}) %collective-permute-start.2) | collective-permute-done | bytes 131104 | tf_op jit(solution)/shard_map/ppermute | solution.py:150
  83.9 0.0 collective-permute-done.1
  83.9 0.0 copy-start.2
  83.9 0.5 collective-permute-start.9
  84.4 1.2 collective-permute-start.7
  85.7 1.0 collective-permute-start.5
  86.7 4.3 %collective-permute-start.4 = (f32[64,512]{1,0:T(8,128)S(1)}, f32[64,512]{1,0:T(8,128)S(1)}, u32[]{:S(2)}, u32[]{:S(2)}) collective-permute-start(f32[64,512]{1,0:T(8,128)S(1)} %add_add_fusion.refs_0_), channel_id=1, source_target_pairs={{0,1},{1,0},{2,3},{3,2},{4,5},{5,4},{6,7},{7,6},{8,9},{9,8},{10,11... | collective-permute-start | bytes 393224 | tf_op jit(solution)/shard_map/ppermute | solution.py:150
  91.0 0.0 collective-permute-done.9.refs_6_
  91.0 2.4 %collective-permute-start.10 = (f32[64,512]{1,0:T(8,128)S(1)}, f32[64,512]{1,0:T(8,128)S(1)}, u32[]{:S(2)}, u32[]{:S(2)}) collective-permute-start(f32[64,512]{1,0:T(8,128)S(1)} %collective-permute-done.9.refs_6_), channel_id=1, source_target_pairs={{0,1},{1,0},{2,3},{3,2},{4,5},{5,4},{6,7},{7,6},{8,9},{9,8},{10,11... | collective-permute-start | bytes 393224 | tf_op jit(solution)/shard_map/ppermute | solution.py:150
  93.3 0.3 collective-permute-start.13
  93.7 0.0 collective-permute-done.7.refs_4_
  93.7 1.0 collective-permute-start.12
  94.7 0.0 collective-permute-done.5.refs_2_
  94.7 0.8 collective-permute-start.11
  95.5 0.0 collective-permute-done.4.refs_1_
  95.5 0.1 collective-permute-start.8
  95.6 0.0 collective-permute-done.10.refs_7_
  95.6 0.4 collective-permute-start.6
  96.0 0.8 collective-permute-done.8.refs_5_
  96.8 0.0 copy-done.5
  96.8 0.0 copy-done.6
  96.8 0.0 copy-done.7
  96.9 0.0 copy-start.8
  96.9 0.6 copy-done.8
  97.5 0.0 collective-permute-done.6.refs_3_
  97.5 0.0 copy-done.4
  97.5 23.9 %factor.1.m_hbm = f32[512,512]{1,0:T(8,128)} custom-call(s32[1]{0:T(128)} %bitcast.pos_ref, f32[64,512]{1,0:T(8,128)} %copy-done.2, f32[64,512]{1,0:T(8,128)} %copy-done.6, f32[64,512]{1,0:T(8,128)} %copy-done.5, f32[64,512]{1,0:T(8,128)} %collective-permute-done.6.refs_3_, f32[64,512]{1,0:T(8,128)} %copy-done.4, f32[64,512]{1,0:T(8,128)} %copy-done.8, ...), custom_call_target="tpu_custom_call" | custom-call | tf_op jit(solution)/shard_map/factor/pallas_call | solution.py:180
  121.4 0.0 collective-permute-done.13
  121.4 0.0 collective-permute-done.12
  121.4 0.0 collective-permute-done.11
  121.4 0.0 all-to-all-done.1
  121.4 0.0 copy-done.1
  121.4 0.0 copy-start
  121.5 1.2 copy-done
  122.7 4.1 %update.1 = (f32[512,512]{1,0:T(8,128)}, f32[512,512]{1,0:T(8,128)}) custom-call(s32[1]{0:T(128)} %bitcast.pos_ref, f32[512,512]{1,0:T(8,128)S(1)} %copy-done, f32[512,512]{1,0:T(8,128)S(1)} %copy-done.1, f32[512,512]{1,0:T(8,128)S(1)} %bitcast.7, f32[8,16,512]{2,1,0:T(8,128)S(1)} %all_to_all.16.refs_0_, f32[8,16,512]{2,1,0:T(8,128)S(1)} %bitcast.13, ...), custom_call_target="tpu_custom_call" | custom-call | tf_op jit(solution)/shard_map/update/pallas_call | solution.py:193
  (11 shorter events, 0.1 us)
Async XLA Ops:
  12.9 108.5 %copy-start.1 = (f32[512,512]{1,0:T(8,128)S(1)}, f32[512,512]{1,0:T(8,128)}, u32[]{:S(2)}) copy-start(f32[512,512]{1,0:T(8,128)} %trail_hbm.1) | copy-start | bytes 3145732
  54.4 67.0 %all-to-all-start.1 = ((f32[8,64,512]{2,1,0:T(8,128)}), f32[8,64,512]{2,1,0:T(8,128)S(1)}, u32[]{:S(2)}, u32[]{:S(2)}) async-start(f32[8,64,512]{2,1,0:T(8,128)} %broadcast_in_dim.4), calls=%async_computation.1 | async-start | bytes 2097152 | tf_op jit(solution)/shard_map/all_to_all | solution.py:141
  58.0 12.3 %collective-permute-start = (f32[64,512]{1,0:T(8,128)}, f32[64,512]{1,0:T(8,128)S(1)}, u32[]{:S(2)}, u32[]{:S(2)}) collective-permute-start(f32[64,512]{1,0:T(8,128)} %get-tuple-element.4), channel_id=1, source_target_pairs={{0,32},{32,0},{64,96},{96,64},{128,160},{160,128},{192,224},{224,1... | collective-permute-start | bytes 393224 | tf_op jit(solution)/shard_map/ppermute | solution.py:150
  71.2 11.0 %collective-permute-start.3 = (f32[64,512]{1,0:T(8,128)S(1)}, f32[64,512]{1,0:T(8,128)S(1)}, u32[]{:S(2)}, u32[]{:S(2)}) collective-permute-start(f32[64,512]{1,0:T(8,128)S(1)} %add.12), channel_id=1, source_target_pairs={{0,192},{32,224},{64,128},{96,160},{128,64},{160,96},{192,0},{224,... | collective-permute-start | bytes 393224 | tf_op jit(solution)/shard_map/ppermute | solution.py:150
  78.5 5.4 %collective-permute-start.2 = (f32[64,512]{1,0:T(8,128)S(1)}, f32[64,512]{1,0:T(8,128)S(1)}, u32[]{:S(2)}, u32[]{:S(2)}) collective-permute-start(f32[64,512]{1,0:T(8,128)S(1)} %add.12), channel_id=1, source_target_pairs={{0,128},{32,160},{64,192},{96,224},{128,0},{160,32},{192,64},{224,... | collective-permute-start | bytes 393224 | tf_op jit(solution)/shard_map/ppermute | solution.py:150
  78.7 5.1 %collective-permute-start.1 = (f32[64,512]{1,0:T(8,128)S(1)}, f32[64,512]{1,0:T(8,128)S(1)}, u32[]{:S(2)}, u32[]{:S(2)}) collective-permute-start(f32[64,512]{1,0:T(8,128)S(1)} %add.12), channel_id=1, source_target_pairs={{0,64},{32,96},{64,0},{96,32},{128,192},{160,224},{192,128},{224,1... | collective-permute-start | bytes 393224 | tf_op jit(solution)/shard_map/ppermute | solution.py:150
  83.9 13.6 %copy-start.2 = (f32[64,512]{1,0:T(8,128)}, f32[64,512]{1,0:T(8,128)S(1)}, u32[]{:S(2)}) copy-start(f32[64,512]{1,0:T(8,128)S(1)} %add_add_fusion.refs_0_) | copy-start | bytes 393220
  83.9 7.0 %collective-permute-start.9 = (f32[64,512]{1,0:T(8,128)S(1)}, f32[64,512]{1,0:T(8,128)S(1)}, u32[]{:S(2)}, u32[]{:S(2)}) collective-permute-start(f32[64,512]{1,0:T(8,128)S(1)} %add_add_fusion.refs_0_), channel_id=1, source_target_pairs={{0,6},{1,7},{2,4},{3,5},{4,2},{5,3},{6,0},{7,1},{8,14},{9,15},{10,... | collective-permute-start | bytes 393224 | tf_op jit(solution)/shard_map/ppermute | solution.py:150
  84.4 9.3 %collective-permute-start.7 = (f32[64,512]{1,0:T(8,128)S(1)}, f32[64,512]{1,0:T(8,128)S(1)}, u32[]{:S(2)}, u32[]{:S(2)}) collective-permute-start(f32[64,512]{1,0:T(8,128)S(1)} %add_add_fusion.refs_0_), channel_id=1, source_target_pairs={{0,4},{1,5},{2,6},{3,7},{4,0},{5,1},{6,2},{7,3},{8,12},{9,13},{10,... | collective-permute-start | bytes 393224 | tf_op jit(solution)/shard_map/ppermute | solution.py:150
  85.7 9.0 %collective-permute-start.5 = (f32[64,512]{1,0:T(8,128)S(1)}, f32[64,512]{1,0:T(8,128)S(1)}, u32[]{:S(2)}, u32[]{:S(2)}) collective-permute-start(f32[64,512]{1,0:T(8,128)S(1)} %add_add_fusion.refs_0_), channel_id=1, source_target_pairs={{0,2},{1,3},{2,0},{3,1},{4,6},{5,7},{6,4},{7,5},{8,10},{9,11},{10,... | collective-permute-start | bytes 393224 | tf_op jit(solution)/shard_map/ppermute | solution.py:150
  86.7 8.8 %collective-permute-start.4 = (f32[64,512]{1,0:T(8,128)S(1)}, f32[64,512]{1,0:T(8,128)S(1)}, u32[]{:S(2)}, u32[]{:S(2)}) collective-permute-start(f32[64,512]{1,0:T(8,128)S(1)} %add_add_fusion.refs_0_), channel_id=1, source_target_pairs={{0,1},{1,0},{2,3},{3,2},{4,5},{5,4},{6,7},{7,6},{8,9},{9,8},{10,11... | collective-permute-start | bytes 393224 | tf_op jit(solution)/shard_map/ppermute | solution.py:150
  91.0 6.6 %copy-start.3 = (f32[64,512]{1,0:T(8,128)}, f32[64,512]{1,0:T(8,128)S(1)}, u32[]{:S(2)}) copy-start(f32[64,512]{1,0:T(8,128)S(1)} %collective-permute-done.9.refs_6_) | copy-start | bytes 393220
  91.0 4.6 %collective-permute-start.10 = (f32[64,512]{1,0:T(8,128)S(1)}, f32[64,512]{1,0:T(8,128)S(1)}, u32[]{:S(2)}, u32[]{:S(2)}) collective-permute-start(f32[64,512]{1,0:T(8,128)S(1)} %collective-permute-done.9.refs_6_), channel_id=1, source_target_pairs={{0,1},{1,0},{2,3},{3,2},{4,5},{5,4},{6,7},{7,6},{8,9},{9,8},{10,11... | collective-permute-start | bytes 393224 | tf_op jit(solution)/shard_map/ppermute | solution.py:150
  93.3 28.1 %collective-permute-start.13 = (f32[128,512]{1,0:T(8,128)S(1)}, f32[128,512]{1,0:T(8,128)S(1)}, u32[]{:S(2)}, u32[]{:S(2)}) collective-permute-start(f32[128,512]{1,0:T(8,128)S(1)} %bitcast.8), channel_id=1, source_target_pairs={{0,3},{1,2},{2,1},{3,0},{4,7},{5,6},{6,5},{7,4},{8,11},{9,10},{10,... | collective-permute-start | bytes 786440 | tf_op jit(solution)/shard_map/ppermute | solution.py:150
  93.7 3.8 %copy-start.4 = (f32[64,512]{1,0:T(8,128)}, f32[64,512]{1,0:T(8,128)S(1)}, u32[]{:S(2)}) copy-start(f32[64,512]{1,0:T(8,128)S(1)} %collective-permute-done.7.refs_4_) | copy-start | bytes 393220
  93.7 27.7 %collective-permute-start.12 = (f32[128,512]{1,0:T(8,128)S(1)}, f32[128,512]{1,0:T(8,128)S(1)}, u32[]{:S(2)}, u32[]{:S(2)}) collective-permute-start(f32[128,512]{1,0:T(8,128)S(1)} %bitcast.9), channel_id=1, source_target_pairs={{0,2},{1,3},{2,0},{3,1},{4,6},{5,7},{6,4},{7,5},{8,10},{9,11},{10,... | collective-permute-start | bytes 786440 | tf_op jit(solution)/shard_map/ppermute | solution.py:150
  94.7 2.1 %copy-start.5 = (f32[64,512]{1,0:T(8,128)}, f32[64,512]{1,0:T(8,128)S(1)}, u32[]{:S(2)}) copy-start(f32[64,512]{1,0:T(8,128)S(1)} %collective-permute-done.5.refs_2_) | copy-start | bytes 393220
  94.7 26.7 %collective-permute-start.11 = (f32[128,512]{1,0:T(8,128)S(1)}, f32[128,512]{1,0:T(8,128)S(1)}, u32[]{:S(2)}, u32[]{:S(2)}) collective-permute-start(f32[128,512]{1,0:T(8,128)S(1)} %bitcast.10), channel_id=1, source_target_pairs={{0,1},{1,0},{2,3},{3,2},{4,5},{5,4},{6,7},{7,6},{8,9},{9,8},{10,11... | collective-permute-start | bytes 786440 | tf_op jit(solution)/shard_map/ppermute | solution.py:150
  95.5 1.4 %copy-start.6 = (f32[64,512]{1,0:T(8,128)}, f32[64,512]{1,0:T(8,128)S(1)}, u32[]{:S(2)}) copy-start(f32[64,512]{1,0:T(8,128)S(1)} %collective-permute-done.4.refs_1_) | copy-start | bytes 393220
  95.5 1.3 %collective-permute-start.8 = (f32[64,512]{1,0:T(8,128)S(1)}, f32[64,512]{1,0:T(8,128)S(1)}, u32[]{:S(2)}, u32[]{:S(2)}) collective-permute-start(f32[64,512]{1,0:T(8,128)S(1)} %collective-permute-done.7.refs_4_), channel_id=1, source_target_pairs={{0,1},{1,0},{2,3},{3,2},{4,5},{5,4},{6,7},{7,6},{8,9},{9,8},{10,11... | collective-permute-start | bytes 393224 | tf_op jit(solution)/shard_map/ppermute | solution.py:150
  95.6 1.2 copy-start.7
  95.6 1.9 %collective-permute-start.6 = (f32[64,512]{1,0:T(8,128)S(1)}, f32[64,512]{1,0:T(8,128)}, u32[]{:S(2)}, u32[]{:S(2)}) collective-permute-start(f32[64,512]{1,0:T(8,128)S(1)} %collective-permute-done.5.refs_2_), channel_id=1, source_target_pairs={{0,1},{1,0},{2,3},{3,2},{4,5},{5,4},{6,7},{7,6},{8,9},{9,8},{10,11... | collective-permute-start | bytes 393224 | tf_op jit(solution)/shard_map/ppermute | solution.py:150
  96.9 0.6 copy-start.8
  121.4 1.2 copy-start

commit v2 on v1

--- a/solution.py
+++ b/solution.py
@@ -116,6 +116,11 @@
             m_ref[hi:, :hi] = m_ref[hi:, :hi] - dot(p, m_ref[lo:hi, :hi], 1, 0)
 
 
+def join_kernel(pos_ref, *refs):
+    for k in range(8):
+        refs[8][(pos_ref[0] >> 2) ^ k] = refs[k][...]
+
+
 def update_kernel(pos_ref, m_hbm, trail_hbm, slab_hbm, *refs):
     panel_ref, out_ref, m_ref, slab_ref, x_ref, trail_ref, sems = refs[4:]
     copies = [pltpu.make_async_copy(slab_hbm, slab_ref, sems.at[4]), pltpu.make_async_copy(m_hbm, m_ref, sems.at[6])]
@@ -137,12 +142,8 @@
     return jax.ShapeDtypeStruct((n, N), jnp.float32)
 
 
-def swap(x, axis, groups=None):
-    return lax.all_to_all(x, axis, split_axis=0, concat_axis=0, axis_index_groups=groups, tiled=True)
-
-
-def gathered(x, axis, groups=None):
-    return swap(jnp.broadcast_to(x[None], (8, *x.shape)), axis, groups).reshape(-1, N)
+def swap(x):
+    return lax.all_to_all(x, "scen", split_axis=0, concat_axis=0, tiled=True)
 
 
 def flip(x, axis, bits):
@@ -168,7 +169,7 @@
         name="product",
     )(pos, factor_rows, panel_factor)
 
-    own = swap(slab.reshape(8, 64, N), "scen")
+    own = swap(slab.reshape(8, 64, N))
     own = own.sum(0)
     gram = gram + flip(gram, "scen", 1)
     gram = (gram + flip(gram, "scen", 2)) + (flip(gram, "scen", 4) + flip(gram, "scen", 6))
@@ -186,10 +187,18 @@
         name="factor",
     )(pos, *pieces, pivot_add)
 
-    column = [[4 * z + k for z in range(8)] for k in range(4)]
-    cross = [gathered(own[:16], "rows", column)]
-    cross += [flip(cross[0], "rows", q) for q in (1, 2, 3)]
-    whole = gathered(own, "scen")
+    column = [own[:16]]
+    column += [flip(column[0], "rows", 4 * k) for k in range(1, 8)]
+    column = pl.pallas_call(
+        join_kernel,
+        out_shape=jax.ShapeDtypeStruct((8, 16, N), jnp.float32),
+        in_specs=[SMEM] + [VMEM] * 8,
+        out_specs=VMEM,
+        compiler_params=pltpu.CompilerParams(vmem_limit_bytes=2 << 20),
+        name="join",
+    )(pos, *column)
+    cross = [column] + [flip(column, "rows", q) for q in (1, 2, 3)]
+    whole = swap(jnp.broadcast_to(own[None], (8, 64, N))).reshape(N, N)
     return pl.pallas_call(
         update_kernel,
         out_shape=(shape(N), shape(N)),
@@ -204,7 +213,7 @@
         ],
         compiler_params=pltpu.CompilerParams(vmem_limit_bytes=28 << 20),
         name="update",
-    )(pos, m, trailing, whole, *[x.reshape(8, 16, N) for x in cross])
+    )(pos, m, trailing, whole, *cross)
 
 
 def solution(mesh):

time: 127 us -> 122 us (0.961)
  blocking collectives: 40.3 us -> 0 us
  starting transfers between devices: 26.4 us -> 48.2 us
  waiting for transfers between devices: 15 us -> 28.6 us
    all_to_all x2 -> x0, blocking collectives: 40.3 us -> none  [swap(): lax.all_to_all(x, axis, split_axis=0, concat_axis=0, axis_index_groups=gr...]
    ppermute x14 -> x21, starting transfers between devices: 22.9 us -> 36.7 us  [flip(): return lax.ppermute(x, axis, [(i, i ^ bits) for i in range(n)])]
    all_to_all x1 -> x2, waiting for transfers between devices: 0.01 us -> 12.7 us  [swap(): return lax.all_to_all(x, 'scen', split_axis=0, concat_axis=0, tiled=True)]
    all_to_all x1 -> x2, starting transfers between devices: 3.56 us -> 11.5 us  [swap(): return lax.all_to_all(x, 'scen', split_axis=0, concat_axis=0, tiled=True)]
    ppermute x14 -> x21, waiting for transfers between devices: 15 us -> 16 us  [flip(): return lax.ppermute(x, axis, [(i, i ^ bits) for i in range(n)])]
  transfers between devices with their start and end apart: 15 -> 23, of which waited for: 4 -> 6; matrix products, arithmetic and copies ran while one was open for 1% -> 2% of each run, Pallas kernels for 19% -> 20%
where the time goes in v2:
time: 122 us
  starting transfers between devices  48.2 us (40%)
  Pallas kernels  40.2 us (33%)
  waiting for transfers between devices  28.6 us (23%)
  local copies, waits for them, and re-layouts  3 us (2%)
    ppermute x21, starting transfers between devices, flip(): return lax.ppermute(x, axis, [(i, i ^ bits) for i in range(n)])  36.7 us
    pallas_call x1, Pallas kernels, per_device(): pl.pallas_call(factor_kernel, out_shape=shape(N), in_specs=[SMEM] + [HBM]...  23.9 us
    ppermute x21, waiting for transfers between devices, flip(): return lax.ppermute(x, axis, [(i, i ^ bits) for i in range(n)])  16 us
    all_to_all x2, waiting for transfers between devices, swap(): return lax.all_to_all(x, 'scen', split_axis=0, concat_axis=0, tiled=True)  12.7 us
    pallas_call x1, Pallas kernels, per_device(): pl.pallas_call(product_kernel, grid=(groups,), out_shape=(shape(N), shape...  12.3 us
    all_to_all x2, starting transfers between devices, swap(): return lax.all_to_all(x, 'scen', split_axis=0, concat_axis=0, tiled=True)  11.5 us
    pallas_call x1, Pallas kernels, per_device(): pl.pallas_call(update_kernel, out_shape=(shape(N), shape(N)), in_specs=[S...  4.1 us
  transfers between devices with their start and end apart: 23, of which 6 were waited for; matrix products, arithmetic and copies ran while one was open for 2% of the time, Pallas kernels for 20%

profile of v2, /device:TPU:1, one launch (start us, length us, event | category | flops | bytes accessed | tf_op | source)
XLA Modules:
  0.0 122.0 jit_solution(9698766444918600519)
XLA Ops:
  0.6 12.3 %product.1 = (f32[512,512]{1,0:T(8,128)}, f32[64,512]{1,0:T(8,128)}) custom-call(s32[1]{0:T(128)} %bitcast.pos_ref, f32[4,512,1024]{2,1,0:T(8,128)} %f_ref.1, f32[4,1024,512]{2,1,0:T(8,128)} %p_ref.1), custom_call_target="tpu_custom_call" | custom-call | tf_op jit(solution)/shard_map/product/pallas_call | solution.py:157
  12.9 7.6 %all-to-all-start = ((f32[8,64,512]{2,1,0:T(8,128)}), f32[8,64,512]{2,1,0:T(8,128)S(1)}, u32[]{:S(2)}, u32[]{:S(2)}) async-start(f32[8,64,512]{2,1,0:T(8,128)} %bitcast.4), calls=%async_computation | async-start | bytes 2097152 | tf_op jit(solution)/shard_map/all_to_all | solution.py:146
  20.5 3.0 %collective-permute-start = (f32[64,512]{1,0:T(8,128)}, f32[64,512]{1,0:T(8,128)S(1)}, u32[]{:S(2)}, u32[]{:S(2)}) collective-permute-start(f32[64,512]{1,0:T(8,128)} %get-tuple-element.4), channel_id=1, source_target_pairs={{0,32},{32,0},{64,96},{96,64},{128,160},{160,128},{192,224},{224,1... | collective-permute-start | bytes 393224 | tf_op jit(solution)/shard_map/ppermute | solution.py:151
  23.5 12.6 %all-to-all-done = f32[8,64,512]{2,1,0:T(8,128)S(1)} async-done(((f32[8,64,512]{2,1,0:T(8,128)}), f32[8,64,512]{2,1,0:T(8,128)S(1)}, u32[]{:S(2)}, u32[]{:S(2)}) %all-to-all-start) | async-done | bytes 1048608 | tf_op jit(solution)/shard_map/all_to_all | solution.py:146
  36.1 0.1 reduce_sum.9
  36.2 1.1 broadcast_in_dim.2
  37.3 3.9 %all-to-all-start.1 = ((f32[8,64,512]{2,1,0:T(8,128)}), f32[8,64,512]{2,1,0:T(8,128)S(1)}, u32[]{:S(2)}, u32[]{:S(2)}) async-start(f32[8,64,512]{2,1,0:T(8,128)} %broadcast_in_dim.2), calls=%async_computation.1 | async-start | bytes 2097152 | tf_op jit(solution)/shard_map/all_to_all | solution.py:146
  41.2 0.9 add.12
  42.1 2.8 %collective-permute-start.3 = (f32[64,512]{1,0:T(8,128)S(1)}, f32[64,512]{1,0:T(8,128)S(1)}, u32[]{:S(2)}, u32[]{:S(2)}) collective-permute-start(f32[64,512]{1,0:T(8,128)S(1)} %add.12), channel_id=1, source_target_pairs={{0,192},{32,224},{64,128},{96,160},{128,64},{160,96},{192,0},{224,... | collective-permute-start | bytes 393224 | tf_op jit(solution)/shard_map/ppermute | solution.py:151
  44.9 0.6 collective-permute-start.2
  45.5 0.1 collective-permute-start.1
  45.6 7.7 %collective-permute-done.3 = f32[64,512]{1,0:T(8,128)S(1)} collective-permute-done((f32[64,512]{1,0:T(8,128)S(1)}, f32[64,512]{1,0:T(8,128)S(1)}, u32[]{:S(2)}, u32[]{:S(2)}) %collective-permute-start.3) | collective-permute-done | bytes 131104 | tf_op jit(solution)/shard_map/ppermute | solution.py:151
  53.3 5.5 %collective-permute-done.2 = f32[64,512]{1,0:T(8,128)S(1)} collective-permute-done((f32[64,512]{1,0:T(8,128)S(1)}, f32[64,512]{1,0:T(8,128)S(1)}, u32[]{:S(2)}, u32[]{:S(2)}) %collective-permute-start.2) | collective-permute-done | bytes 131104 | tf_op jit(solution)/shard_map/ppermute | solution.py:151
  58.7 0.4 collective-permute-done.1
  59.2 2.0 %collective-permute-start.9 = (f32[64,512]{1,0:T(8,128)S(1)}, f32[64,512]{1,0:T(8,128)S(1)}, u32[]{:S(2)}, u32[]{:S(2)}) collective-permute-start(f32[64,512]{1,0:T(8,128)S(1)} %add_add_fusion.refs_0_), channel_id=1, source_target_pairs={{0,6},{1,7},{2,4},{3,5},{4,2},{5,3},{6,0},{7,1},{8,14},{9,15},{10,... | collective-permute-start | bytes 393224 | tf_op jit(solution)/shard_map/ppermute | solution.py:151
  61.2 1.0 collective-permute-start.5
  62.2 5.4 %collective-permute-start.17 = (f32[16,512]{1,0:T(8,128)S(1)}, f32[16,512]{1,0:T(8,128)S(1)}, u32[]{:S(2)}, u32[]{:S(2)}) collective-permute-start(f32[16,512]{1,0:T(8,128)S(1)} %slice.4.refs_0_), channel_id=1, source_target_pairs={{0,28},{1,29},{2,30},{3,31},{4,24},{5,25},{6,26},{7,27},{8,20},{9,... | collective-permute-start | bytes 98312 | tf_op jit(solution)/shard_map/ppermute | solution.py:151
  67.6 0.3 collective-permute-start.16
  68.0 3.6 %collective-permute-start.15 = (f32[16,512]{1,0:T(8,128)S(1)}, f32[16,512]{1,0:T(8,128)S(1)}, u32[]{:S(2)}, u32[]{:S(2)}) collective-permute-start(f32[16,512]{1,0:T(8,128)S(1)} %slice.4.refs_0_), channel_id=1, source_target_pairs={{0,20},{1,21},{2,22},{3,23},{4,16},{5,17},{6,18},{7,19},{8,28},{9,... | collective-permute-start | bytes 98312 | tf_op jit(solution)/shard_map/ppermute | solution.py:151
  71.5 0.0 collective-permute-done.17.refs_7_
  71.5 1.9 %collective-permute-start.14 = (f32[16,512]{1,0:T(8,128)S(1)}, f32[16,512]{1,0:T(8,128)S(1)}, u32[]{:S(2)}, u32[]{:S(2)}) collective-permute-start(f32[16,512]{1,0:T(8,128)S(1)} %slice.4.refs_0_), channel_id=1, source_target_pairs={{0,16},{1,17},{2,18},{3,19},{4,20},{5,21},{6,22},{7,23},{8,24},{9,... | collective-permute-start | bytes 98312 | tf_op jit(solution)/shard_map/ppermute | solution.py:151
  73.4 0.0 collective-permute-done.16.refs_6_
  73.4 1.7 %collective-permute-start.13 = (f32[16,512]{1,0:T(8,128)S(1)}, f32[16,512]{1,0:T(8,128)S(1)}, u32[]{:S(2)}, u32[]{:S(2)}) collective-permute-start(f32[16,512]{1,0:T(8,128)S(1)} %slice.4.refs_0_), channel_id=1, source_target_pairs={{0,12},{1,13},{2,14},{3,15},{4,8},{5,9},{6,10},{7,11},{8,4},{9,5},... | collective-permute-start | bytes 98312 | tf_op jit(solution)/shard_map/ppermute | solution.py:151
  75.2 0.0 collective-permute-done.15.refs_5_
  75.2 1.8 %collective-permute-start.12 = (f32[16,512]{1,0:T(8,128)S(1)}, f32[16,512]{1,0:T(8,128)S(1)}, u32[]{:S(2)}, u32[]{:S(2)}) collective-permute-start(f32[16,512]{1,0:T(8,128)S(1)} %slice.4.refs_0_), channel_id=1, source_target_pairs={{0,8},{1,9},{2,10},{3,11},{4,12},{5,13},{6,14},{7,15},{8,0},{9,1},... | collective-permute-start | bytes 98312 | tf_op jit(solution)/shard_map/ppermute | solution.py:151
  77.0 1.2 %collective-permute-done.14.refs_4_ = f32[16,512]{1,0:T(8,128)S(1)} collective-permute-done((f32[16,512]{1,0:T(8,128)S(1)}, f32[16,512]{1,0:T(8,128)S(1)}, u32[]{:S(2)}, u32[]{:S(2)}) %collective-permute-start.14) | collective-permute-done | bytes 32800 | tf_op jit(solution)/shard_map/ppermute | solution.py:151
  78.2 2.5 %collective-permute-start.11 = (f32[16,512]{1,0:T(8,128)S(1)}, f32[16,512]{1,0:T(8,128)S(1)}, u32[]{:S(2)}, u32[]{:S(2)}) collective-permute-start(f32[16,512]{1,0:T(8,128)S(1)} %slice.4.refs_0_), channel_id=1, source_target_pairs={{0,4},{1,5},{2,6},{3,7},{4,0},{5,1},{6,2},{7,3},{8,12},{9,13},{10,... | collective-permute-start | bytes 98312 | tf_op jit(solution)/shard_map/ppermute | solution.py:151
  80.8 0.0 collective-permute-done.13.refs_3_
  80.8 6.1 %collective-permute-start.4 = (f32[64,512]{1,0:T(8,128)S(1)}, f32[64,512]{1,0:T(8,128)S(1)}, u32[]{:S(2)}, u32[]{:S(2)}) collective-permute-start(f32[64,512]{1,0:T(8,128)S(1)} %add_add_fusion.refs_0_), channel_id=1, source_target_pairs={{0,1},{1,0},{2,3},{3,2},{4,5},{5,4},{6,7},{7,6},{8,9},{9,8},{10,11... | collective-permute-start | bytes 393224 | tf_op jit(solution)/shard_map/ppermute | solution.py:151
  86.8 0.0 collective-permute-done.12.refs_2_
  86.8 0.1 collective-permute-start.10
  86.9 0.0 collective-permute-done.11.refs_1_
  87.0 2.2 %collective-permute-start.20 = (f32[8,16,512]{2,1,0:T(8,128)S(1)}, f32[8,16,512]{2,1,0:T(8,128)S(1)}, u32[]{:S(2)}, u32[]{:S(2)}) collective-permute-start(f32[8,16,512]{2,1,0:T(8,128)S(1)} %join.1.refs_0_), channel_id=1, source_target_pairs={{0,3},{1,2},{2,1},{3,0},{4,7},{5,6},{6,5},{7,4},{8,11},{9,10},{10,... | collective-permute-start | bytes 786440 | tf_op jit(solution)/shard_map/ppermute | solution.py:151
  89.2 1.0 collective-permute-start.19
  90.2 0.0 collective-permute-done.4.refs_1_
  90.2 0.5 collective-permute-start.8
  90.7 0.0 collective-permute-done.10.refs_7_
  90.7 0.1 collective-permute-start.6
  90.8 1.1 collective-permute-done.8.refs_5_
  91.9 0.7 copy-done.8
  92.6 0.0 collective-permute-done.6.refs_3_
  92.6 23.9 %factor.1.m_hbm = f32[512,512]{1,0:T(8,128)} custom-call(s32[1]{0:T(128)} %bitcast.pos_ref, f32[64,512]{1,0:T(8,128)} %copy-done.2, f32[64,512]{1,0:T(8,128)} %copy-done.6, f32[64,512]{1,0:T(8,128)} %copy-done.5, f32[64,512]{1,0:T(8,128)} %collective-permute-done.6.refs_3_, f32[64,512]{1,0:T(8,128)} %copy-done.4, f32[64,512]{1,0:T(8,128)} %copy-done.8, ...), custom_call_target="tpu_custom_call" | custom-call | tf_op jit(solution)/shard_map/factor/pallas_call | solution.py:181
  116.5 0.0 collective-permute-done.20.refs_3_
  116.5 0.0 collective-permute-done.18.refs_1_
  116.5 0.0 all-to-all-done.1
  116.5 0.0 copy-start
  116.6 1.2 copy-done
  117.8 4.1 %update.1 = (f32[512,512]{1,0:T(8,128)}, f32[512,512]{1,0:T(8,128)}) custom-call(s32[1]{0:T(128)} %bitcast.pos_ref, f32[512,512]{1,0:T(8,128)S(1)} %copy-done, f32[512,512]{1,0:T(8,128)S(1)} %copy-done.1, f32[512,512]{1,0:T(8,128)S(1)} %bitcast.3, f32[8,16,512]{2,1,0:T(8,128)S(1)} %join.1.refs_0_, f32[8,16,512]{2,1,0:T(8,128)S(1)} %collective-permute-done.18.refs_1_, ...), custom_call_target="tpu_custom_call" | custom-call | tf_op jit(solution)/shard_map/update/pallas_call | solution.py:202
  (25 shorter events, 0.1 us)
Async XLA Ops:
  12.9 103.6 %copy-start.1 = (f32[512,512]{1,0:T(8,128)S(1)}, f32[512,512]{1,0:T(8,128)}, u32[]{:S(2)}) copy-start(f32[512,512]{1,0:T(8,128)} %trail_hbm.1) | copy-start | bytes 3145732
  12.9 23.2 %all-to-all-start = ((f32[8,64,512]{2,1,0:T(8,128)}), f32[8,64,512]{2,1,0:T(8,128)S(1)}, u32[]{:S(2)}, u32[]{:S(2)}) async-start(f32[8,64,512]{2,1,0:T(8,128)} %bitcast.4), calls=%async_computation | async-start | bytes 2097152 | tf_op jit(solution)/shard_map/all_to_all | solution.py:146
  20.5 20.7 %collective-permute-start = (f32[64,512]{1,0:T(8,128)}, f32[64,512]{1,0:T(8,128)S(1)}, u32[]{:S(2)}, u32[]{:S(2)}) collective-permute-start(f32[64,512]{1,0:T(8,128)} %get-tuple-element.4), channel_id=1, source_target_pairs={{0,32},{32,0},{64,96},{96,64},{128,160},{160,128},{192,224},{224,1... | collective-permute-start | bytes 393224 | tf_op jit(solution)/shard_map/ppermute | solution.py:151
  37.3 79.2 %all-to-all-start.1 = ((f32[8,64,512]{2,1,0:T(8,128)}), f32[8,64,512]{2,1,0:T(8,128)S(1)}, u32[]{:S(2)}, u32[]{:S(2)}) async-start(f32[8,64,512]{2,1,0:T(8,128)} %broadcast_in_dim.2), calls=%async_computation.1 | async-start | bytes 2097152 | tf_op jit(solution)/shard_map/all_to_all | solution.py:146
  42.1 11.1 %collective-permute-start.3 = (f32[64,512]{1,0:T(8,128)S(1)}, f32[64,512]{1,0:T(8,128)S(1)}, u32[]{:S(2)}, u32[]{:S(2)}) collective-permute-start(f32[64,512]{1,0:T(8,128)S(1)} %add.12), channel_id=1, source_target_pairs={{0,192},{32,224},{64,128},{96,160},{128,64},{160,96},{192,0},{224,... | collective-permute-start | bytes 393224 | tf_op jit(solution)/shard_map/ppermute | solution.py:151
  44.9 13.9 %collective-permute-start.2 = (f32[64,512]{1,0:T(8,128)S(1)}, f32[64,512]{1,0:T(8,128)S(1)}, u32[]{:S(2)}, u32[]{:S(2)}) collective-permute-start(f32[64,512]{1,0:T(8,128)S(1)} %add.12), channel_id=1, source_target_pairs={{0,128},{32,160},{64,192},{96,224},{128,0},{160,32},{192,64},{224,... | collective-permute-start | bytes 393224 | tf_op jit(solution)/shard_map/ppermute | solution.py:151
  45.5 13.7 %collective-permute-start.1 = (f32[64,512]{1,0:T(8,128)S(1)}, f32[64,512]{1,0:T(8,128)S(1)}, u32[]{:S(2)}, u32[]{:S(2)}) collective-permute-start(f32[64,512]{1,0:T(8,128)S(1)} %add.12), channel_id=1, source_target_pairs={{0,64},{32,96},{64,0},{96,32},{128,192},{160,224},{192,128},{224,1... | collective-permute-start | bytes 393224 | tf_op jit(solution)/shard_map/ppermute | solution.py:151
  59.2 33.4 %copy-start.2 = (f32[64,512]{1,0:T(8,128)}, f32[64,512]{1,0:T(8,128)S(1)}, u32[]{:S(2)}) copy-start(f32[64,512]{1,0:T(8,128)S(1)} %add_add_fusion.refs_0_) | copy-start | bytes 393220
  59.2 8.8 %collective-permute-start.9 = (f32[64,512]{1,0:T(8,128)S(1)}, f32[64,512]{1,0:T(8,128)S(1)}, u32[]{:S(2)}, u32[]{:S(2)}) collective-permute-start(f32[64,512]{1,0:T(8,128)S(1)} %add_add_fusion.refs_0_), channel_id=1, source_target_pairs={{0,6},{1,7},{2,4},{3,5},{4,2},{5,3},{6,0},{7,1},{8,14},{9,15},{10,... | collective-permute-start | bytes 393224 | tf_op jit(solution)/shard_map/ppermute | solution.py:151
  61.2 28.0 %collective-permute-start.7 = (f32[64,512]{1,0:T(8,128)S(1)}, f32[64,512]{1,0:T(8,128)S(1)}, u32[]{:S(2)}, u32[]{:S(2)}) collective-permute-start(f32[64,512]{1,0:T(8,128)S(1)} %add_add_fusion.refs_0_), channel_id=1, source_target_pairs={{0,4},{1,5},{2,6},{3,7},{4,0},{5,1},{6,2},{7,3},{8,12},{9,13},{10,... | collective-permute-start | bytes 393224 | tf_op jit(solution)/shard_map/ppermute | solution.py:151
  61.2 29.0 %collective-permute-start.5 = (f32[64,512]{1,0:T(8,128)S(1)}, f32[64,512]{1,0:T(8,128)S(1)}, u32[]{:S(2)}, u32[]{:S(2)}) collective-permute-start(f32[64,512]{1,0:T(8,128)S(1)} %add_add_fusion.refs_0_), channel_id=1, source_target_pairs={{0,2},{1,3},{2,0},{3,1},{4,6},{5,7},{6,4},{7,5},{8,10},{9,11},{10,... | collective-permute-start | bytes 393224 | tf_op jit(solution)/shard_map/ppermute | solution.py:151
  62.2 9.3 %collective-permute-start.17 = (f32[16,512]{1,0:T(8,128)S(1)}, f32[16,512]{1,0:T(8,128)S(1)}, u32[]{:S(2)}, u32[]{:S(2)}) collective-permute-start(f32[16,512]{1,0:T(8,128)S(1)} %slice.4.refs_0_), channel_id=1, source_target_pairs={{0,28},{1,29},{2,30},{3,31},{4,24},{5,25},{6,26},{7,27},{8,20},{9,... | collective-permute-start | bytes 98312 | tf_op jit(solution)/shard_map/ppermute | solution.py:151
  67.6 5.8 %collective-permute-start.16 = (f32[16,512]{1,0:T(8,128)S(1)}, f32[16,512]{1,0:T(8,128)S(1)}, u32[]{:S(2)}, u32[]{:S(2)}) collective-permute-start(f32[16,512]{1,0:T(8,128)S(1)} %slice.4.refs_0_), channel_id=1, source_target_pairs={{0,24},{1,25},{2,26},{3,27},{4,28},{5,29},{6,30},{7,31},{8,16},{9,... | collective-permute-start | bytes 98312 | tf_op jit(solution)/shard_map/ppermute | solution.py:151
  68.0 24.6 %copy-start.3 = (f32[64,512]{1,0:T(8,128)}, f32[64,512]{1,0:T(8,128)S(1)}, u32[]{:S(2)}) copy-start(f32[64,512]{1,0:T(8,128)S(1)} %collective-permute-done.9.refs_6_) | copy-start | bytes 393220
  68.0 7.2 %collective-permute-start.15 = (f32[16,512]{1,0:T(8,128)S(1)}, f32[16,512]{1,0:T(8,128)S(1)}, u32[]{:S(2)}, u32[]{:S(2)}) collective-permute-start(f32[16,512]{1,0:T(8,128)S(1)} %slice.4.refs_0_), channel_id=1, source_target_pairs={{0,20},{1,21},{2,22},{3,23},{4,16},{5,17},{6,18},{7,19},{8,28},{9,... | collective-permute-start | bytes 98312 | tf_op jit(solution)/shard_map/ppermute | solution.py:151
  71.5 6.7 %collective-permute-start.14 = (f32[16,512]{1,0:T(8,128)S(1)}, f32[16,512]{1,0:T(8,128)S(1)}, u32[]{:S(2)}, u32[]{:S(2)}) collective-permute-start(f32[16,512]{1,0:T(8,128)S(1)} %slice.4.refs_0_), channel_id=1, source_target_pairs={{0,16},{1,17},{2,18},{3,19},{4,20},{5,21},{6,22},{7,23},{8,24},{9,... | collective-permute-start | bytes 98312 | tf_op jit(solution)/shard_map/ppermute | solution.py:151
  73.4 7.3 %collective-permute-start.13 = (f32[16,512]{1,0:T(8,128)S(1)}, f32[16,512]{1,0:T(8,128)S(1)}, u32[]{:S(2)}, u32[]{:S(2)}) collective-permute-start(f32[16,512]{1,0:T(8,128)S(1)} %slice.4.refs_0_), channel_id=1, source_target_pairs={{0,12},{1,13},{2,14},{3,15},{4,8},{5,9},{6,10},{7,11},{8,4},{9,5},... | collective-permute-start | bytes 98312 | tf_op jit(solution)/shard_map/ppermute | solution.py:151
  75.2 11.7 %collective-permute-start.12 = (f32[16,512]{1,0:T(8,128)S(1)}, f32[16,512]{1,0:T(8,128)S(1)}, u32[]{:S(2)}, u32[]{:S(2)}) collective-permute-start(f32[16,512]{1,0:T(8,128)S(1)} %slice.4.refs_0_), channel_id=1, source_target_pairs={{0,8},{1,9},{2,10},{3,11},{4,12},{5,13},{6,14},{7,15},{8,0},{9,1},... | collective-permute-start | bytes 98312 | tf_op jit(solution)/shard_map/ppermute | solution.py:151
  78.2 8.7 %collective-permute-start.11 = (f32[16,512]{1,0:T(8,128)S(1)}, f32[16,512]{1,0:T(8,128)S(1)}, u32[]{:S(2)}, u32[]{:S(2)}) collective-permute-start(f32[16,512]{1,0:T(8,128)S(1)} %slice.4.refs_0_), channel_id=1, source_target_pairs={{0,4},{1,5},{2,6},{3,7},{4,0},{5,1},{6,2},{7,3},{8,12},{9,13},{10,... | collective-permute-start | bytes 98312 | tf_op jit(solution)/shard_map/ppermute | solution.py:151
  80.8 9.4 %collective-permute-start.4 = (f32[64,512]{1,0:T(8,128)S(1)}, f32[64,512]{1,0:T(8,128)S(1)}, u32[]{:S(2)}, u32[]{:S(2)}) collective-permute-start(f32[64,512]{1,0:T(8,128)S(1)} %add_add_fusion.refs_0_), channel_id=1, source_target_pairs={{0,1},{1,0},{2,3},{3,2},{4,5},{5,4},{6,7},{7,6},{8,9},{9,8},{10,11... | collective-permute-start | bytes 393224 | tf_op jit(solution)/shard_map/ppermute | solution.py:151
  86.8 3.9 %collective-permute-start.10 = (f32[64,512]{1,0:T(8,128)S(1)}, f32[64,512]{1,0:T(8,128)S(1)}, u32[]{:S(2)}, u32[]{:S(2)}) collective-permute-start(f32[64,512]{1,0:T(8,128)S(1)} %collective-permute-done.9.refs_6_), channel_id=1, source_target_pairs={{0,1},{1,0},{2,3},{3,2},{4,5},{5,4},{6,7},{7,6},{8,9},{9,8},{10,11... | collective-permute-start | bytes 393224 | tf_op jit(solution)/shard_map/ppermute | solution.py:151
  87.0 29.5 %collective-permute-start.20 = (f32[8,16,512]{2,1,0:T(8,128)S(1)}, f32[8,16,512]{2,1,0:T(8,128)S(1)}, u32[]{:S(2)}, u32[]{:S(2)}) collective-permute-start(f32[8,16,512]{2,1,0:T(8,128)S(1)} %join.1.refs_0_), channel_id=1, source_target_pairs={{0,3},{1,2},{2,1},{3,0},{4,7},{5,6},{6,5},{7,4},{8,11},{9,10},{10,... | collective-permute-start | bytes 786440 | tf_op jit(solution)/shard_map/ppermute | solution.py:151
  89.2 3.4 %copy-start.4 = (f32[64,512]{1,0:T(8,128)}, f32[64,512]{1,0:T(8,128)S(1)}, u32[]{:S(2)}) copy-start(f32[64,512]{1,0:T(8,128)S(1)} %collective-permute-done.7.refs_4_) | copy-start | bytes 393220
  89.2 27.3 %collective-permute-start.19 = (f32[8,16,512]{2,1,0:T(8,128)S(1)}, f32[8,16,512]{2,1,0:T(8,128)S(1)}, u32[]{:S(2)}, u32[]{:S(2)}) collective-permute-start(f32[8,16,512]{2,1,0:T(8,128)S(1)} %join.1.refs_0_), channel_id=1, source_target_pairs={{0,2},{1,3},{2,0},{3,1},{4,6},{5,7},{6,4},{7,5},{8,10},{9,11},{10,... | collective-permute-start | bytes 786440 | tf_op jit(solution)/shard_map/ppermute | solution.py:151
  90.2 1.7 %copy-start.5 = (f32[64,512]{1,0:T(8,128)}, f32[64,512]{1,0:T(8,128)S(1)}, u32[]{:S(2)}) copy-start(f32[64,512]{1,0:T(8,128)S(1)} %collective-permute-done.5.refs_2_) | copy-start | bytes 393220
  90.2 26.3 %collective-permute-start.18 = (f32[8,16,512]{2,1,0:T(8,128)S(1)}, f32[8,16,512]{2,1,0:T(8,128)S(1)}, u32[]{:S(2)}, u32[]{:S(2)}) collective-permute-start(f32[8,16,512]{2,1,0:T(8,128)S(1)} %join.1.refs_0_), channel_id=1, source_target_pairs={{0,1},{1,0},{2,3},{3,2},{4,5},{5,4},{6,7},{7,6},{8,9},{9,8},{10,11... | collective-permute-start | bytes 786440 | tf_op jit(solution)/shard_map/ppermute | solution.py:151
  90.2 1.7 %copy-start.6 = (f32[64,512]{1,0:T(8,128)}, f32[64,512]{1,0:T(8,128)S(1)}, u32[]{:S(2)}) copy-start(f32[64,512]{1,0:T(8,128)S(1)} %collective-permute-done.4.refs_1_) | copy-start | bytes 393220
  90.2 1.7 %collective-permute-start.8 = (f32[64,512]{1,0:T(8,128)S(1)}, f32[64,512]{1,0:T(8,128)S(1)}, u32[]{:S(2)}, u32[]{:S(2)}) collective-permute-start(f32[64,512]{1,0:T(8,128)S(1)} %collective-permute-done.7.refs_4_), channel_id=1, source_target_pairs={{0,1},{1,0},{2,3},{3,2},{4,5},{5,4},{6,7},{7,6},{8,9},{9,8},{10,11... | collective-permute-start | bytes 393224 | tf_op jit(solution)/shard_map/ppermute | solution.py:151
  90.7 1.2 copy-start.7
  90.7 1.9 %collective-permute-start.6 = (f32[64,512]{1,0:T(8,128)S(1)}, f32[64,512]{1,0:T(8,128)}, u32[]{:S(2)}, u32[]{:S(2)}) collective-permute-start(f32[64,512]{1,0:T(8,128)S(1)} %collective-permute-done.5.refs_2_), channel_id=1, source_target_pairs={{0,1},{1,0},{2,3},{3,2},{4,5},{5,4},{6,7},{7,6},{8,9},{9,8},{10,11... | collective-permute-start | bytes 393224 | tf_op jit(solution)/shard_map/ppermute | solution.py:151
  91.9 0.7 copy-start.8
  116.5 1.2 %copy-start = (f32[512,512]{1,0:T(8,128)S(1)}, f32[512,512]{1,0:T(8,128)}, u32[]{:S(2)}) copy-start(f32[512,512]{1,0:T(8,128)} %factor.1.m_hbm) | copy-start | bytes 3145732

commit v3 on v2

--- a/solution.py
+++ b/solution.py
@@ -71,20 +71,23 @@
     return one(a[0], b[0]) + (one(a[0], b[1]) + one(a[1], b[0]))
 
 
-def product_kernel(pos_ref, f_ref, p_ref, slab_ref, gram_ref, acc_ref):
+def product_kernel(pos_ref, f_ref, p_ref, first_ref, rest_ref, gram_ref, acc_ref, part_ref):
     piece = pos_ref[0] & 7
 
     @pl.when(pl.program_id(0) == 0)
     def _():
         acc_ref[...] = jnp.zeros(acc_ref.shape, jnp.float32)
 
-    part = p_ref[0, :, pl.ds(pl.multiple_of(128 * (piece >> 1), 128), 128)].T
+    part_ref[...] = p_ref[0, :, pl.ds(pl.multiple_of(128 * (piece >> 1), 128), 128)].T
+    part = part_ref[pl.ds(pl.multiple_of(64 * (piece & 1), 64), 64), :]
     acc_ref[...] += dot3(halves(jnp.concatenate([f_ref[0], part], axis=0)), halves(p_ref[0]), 1, 0)
 
     @pl.when(pl.program_id(0) == pl.num_programs(0) - 1)
     def _():
-        slab_ref[...] = acc_ref[:N]
-        gram_ref[...] = acc_ref[pl.ds(pl.multiple_of(N + 64 * (piece & 1), 64), 64), :]
+        for k in range(8):
+            first_ref[k] = acc_ref[64 * k : 64 * k + 16]
+            rest_ref[k] = acc_ref[64 * k + 16 : 64 * k + 64]
+        gram_ref[...] = acc_ref[N:]
 
 
 def factor_kernel(pos_ref, *refs):
@@ -154,23 +157,29 @@
 def per_device(factor_rows, panel_factor, pivot_add, trailing):
     groups, depth, _ = panel_factor.shape
     pos = lax.axis_index("rows").astype(jnp.int32).reshape(1)
-    slab, gram = pl.pallas_call(
+    first, rest, gram = pl.pallas_call(
         product_kernel,
         grid=(groups,),
-        out_shape=(shape(N), shape(64)),
+        out_shape=(jax.ShapeDtypeStruct((8, 16, N), jnp.float32), jax.ShapeDtypeStruct((8, 48, N), jnp.float32), shape(64)),
         in_specs=[
             SMEM,
             pl.BlockSpec((1, N, depth), lambda g: (g, 0, 0)),
             pl.BlockSpec((1, depth, N), lambda g: (g, 0, 0)),
         ],
-        out_specs=(pl.BlockSpec((N, N), lambda g: (0, 0)), pl.BlockSpec((64, N), lambda g: (0, 0))),
-        scratch_shapes=[pltpu.VMEM((N + 128, N), jnp.float32)],
+        out_specs=(
+            pl.BlockSpec((8, 16, N), lambda g: (0, 0, 0)),
+            pl.BlockSpec((8, 48, N), lambda g: (0, 0, 0)),
+            pl.BlockSpec((64, N), lambda g: (0, 0)),
+        ),
+        scratch_shapes=[pltpu.VMEM((N + 64, N), jnp.float32), pltpu.VMEM((128, depth), jnp.float32)],
         compiler_params=pltpu.CompilerParams(vmem_limit_bytes=56 << 20),
         name="product",
     )(pos, factor_rows, panel_factor)
 
-    own = swap(slab.reshape(8, 64, N))
-    own = own.sum(0)
+    first = swap(first)
+    first = lax.optimization_barrier(first.sum(0))
+    rest = swap(rest)
+    rest = lax.optimization_barrier(rest.sum(0))
     gram = gram + flip(gram, "scen", 1)
     gram = (gram + flip(gram, "scen", 2)) + (flip(gram, "scen", 4) + flip(gram, "scen", 6))
     near = [gram]
@@ -187,7 +196,7 @@
         name="factor",
     )(pos, *pieces, pivot_add)
 
-    column = [own[:16]]
+    column = [first]
     column += [flip(column[0], "rows", 4 * k) for k in range(1, 8)]
     column = pl.pallas_call(
         join_kernel,
@@ -198,6 +207,7 @@
         name="join",
     )(pos, *column)
     cross = [column] + [flip(column, "rows", q) for q in (1, 2, 3)]
+    own = jnp.concatenate([first, rest], axis=0)
     whole = swap(jnp.broadcast_to(own[None], (8, 64, N))).reshape(N, N)
     return pl.pallas_call(
         update_kernel,

time: 122 us -> 139 us (1.14)
  blocking collectives: 0 us -> 15 us
  waiting for transfers between devices: 28.6 us -> 32.5 us
  starting transfers between devices: 48.2 us -> 46.5 us
    all_to_all x0 -> x1, blocking collectives: none -> 15 us  [swap(): return lax.all_to_all(x, 'scen', split_axis=0, concat_axis=0, tiled=True)]
    ppermute x21, waiting for transfers between devices: 16 us -> 20.9 us  [flip(): return lax.ppermute(x, axis, [(i, i ^ bits) for i in range(n)])]
    all_to_all x2, starting transfers between devices: 11.5 us -> 8.57 us  [swap(): return lax.all_to_all(x, 'scen', split_axis=0, concat_axis=0, tiled=True)]
  transfers between devices with their start and end apart: 23 -> 23, of which waited for: 6 -> 7; matrix products, arithmetic and copies ran while one was open for 2% -> 1% of each run, Pallas kernels for 20% -> 17%
where the time goes in v3:
time: 139 us
  starting transfers between devices  46.5 us (33%)
  Pallas kernels  39.7 us (29%)
  waiting for transfers between devices  32.5 us (23%)
  blocking collectives  15 us (11%)
  local copies, waits for them, and re-layouts  2.98 us (2%)
    ppermute x21, starting transfers between devices, flip(): return lax.ppermute(x, axis, [(i, i ^ bits) for i in range(n)])  37.9 us
    pallas_call x1, Pallas kernels, per_device(): pl.pallas_call(factor_kernel, out_shape=shape(N), in_specs=[SMEM] + [HBM]...  23.9 us
    ppermute x21, waiting for transfers between devices, flip(): return lax.ppermute(x, axis, [(i, i ^ bits) for i in range(n)])  20.9 us
    all_to_all x1, blocking collectives, swap(): return lax.all_to_all(x, 'scen', split_axis=0, concat_axis=0, tiled=True)  15 us
    pallas_call x1, Pallas kernels, per_device(): pl.pallas_call(product_kernel, grid=(groups,), out_shape=(jax.ShapeDtypeS...  11.7 us
    all_to_all x2, waiting for transfers between devices, swap(): return lax.all_to_all(x, 'scen', split_axis=0, concat_axis=0, tiled=True)  11.6 us
    all_to_all x2, starting transfers between devices, swap(): return lax.all_to_all(x, 'scen', split_axis=0, concat_axis=0, tiled=True)  8.57 us
    pallas_call x1, Pallas kernels, per_device(): pl.pallas_call(update_kernel, out_shape=(shape(N), shape(N)), in_specs=[S...  4.1 us
  transfers between devices with their start and end apart: 23, of which 7 were waited for; matrix products, arithmetic and copies ran while one was open for 1% of the time, Pallas kernels for 17%

profile of v3, /device:TPU:1, one launch (start us, length us, event | category | flops | bytes accessed | tf_op | source)
XLA Modules:
  0.0 138.7 jit_solution(15271538585944679945)
XLA Ops:
  0.6 11.7 %product.1 = (f32[8,16,512]{2,1,0:T(8,128)}, f32[8,48,512]{2,1,0:T(8,128)}, f32[64,512]{1,0:T(8,128)}) custom-call(s32[1]{0:T(128)} %bitcast.pos_ref, f32[4,512,1024]{2,1,0:T(8,128)} %f_ref.1, f32[4,1024,512]{2,1,0:T(8,128)} %p_ref.1), custom_call_target="tpu_custom_call" | custom-call | tf_op jit(solution)/shard_map/product/pallas_call | solution.py:160
  12.3 15.0 %all_to_all.15 = f32[8,16,512]{2,1,0:T(8,128)S(1)} all-to-all(f32[8,16,512]{2,1,0:T(8,128)} %get-tuple-element.6), channel_id=1, replica_groups=mesh['scen'=8,'rows'=32] {'scen'}, dimensions={0} | all-to-all | bytes 524288 | tf_op jit(solution)/shard_map/all_to_all | solution.py:149
  27.4 3.5 %all-to-all-start.1 = ((f32[8,48,512]{2,1,0:T(8,128)}), f32[8,48,512]{2,1,0:T(8,128)S(1)}, u32[]{:S(2)}, u32[]{:S(2)}) async-start(f32[8,48,512]{2,1,0:T(8,128)} %get-tuple-element.7), calls=%async_computation.1 | async-start | bytes 1572864 | tf_op jit(solution)/shard_map/all_to_all | solution.py:149
  30.9 11.6 %all-to-all-done.1 = f32[8,48,512]{2,1,0:T(8,128)S(1)} async-done(((f32[8,48,512]{2,1,0:T(8,128)}), f32[8,48,512]{2,1,0:T(8,128)S(1)}, u32[]{:S(2)}, u32[]{:S(2)}) %all-to-all-start.1) | async-done | bytes 786464 | tf_op jit(solution)/shard_map/all_to_all | solution.py:149
  42.5 0.1 reduce_sum.19
  42.6 1.1 broadcast_in_dim.2
  43.7 5.0 %all-to-all-start.2 = ((f32[8,64,512]{2,1,0:T(8,128)}), f32[8,64,512]{2,1,0:T(8,128)S(1)}, u32[]{:S(2)}, u32[]{:S(2)}) async-start(f32[8,64,512]{2,1,0:T(8,128)} %broadcast_in_dim.2), calls=%async_computation.2 | async-start | bytes 2097152 | tf_op jit(solution)/shard_map/all_to_all | solution.py:149
  48.7 3.0 %collective-permute-start = (f32[64,512]{1,0:T(8,128)}, f32[64,512]{1,0:T(8,128)S(1)}, u32[]{:S(2)}, u32[]{:S(2)}) collective-permute-start(f32[64,512]{1,0:T(8,128)} %get-tuple-element.5), channel_id=1, source_target_pairs={{0,32},{32,0},{64,96},{96,64},{128,160},{160,128},{192,224},{224,1... | collective-permute-start | bytes 393224 | tf_op jit(solution)/shard_map/ppermute | solution.py:154
  51.7 13.6 %collective-permute-done = f32[64,512]{1,0:T(8,128)S(1)} collective-permute-done((f32[64,512]{1,0:T(8,128)}, f32[64,512]{1,0:T(8,128)S(1)}, u32[]{:S(2)}, u32[]{:S(2)}) %collective-permute-start) | collective-permute-done | bytes 131104 | tf_op jit(solution)/shard_map/ppermute | solution.py:154
  65.2 0.9 add.12
  66.1 3.4 %collective-permute-start.3 = (f32[64,512]{1,0:T(8,128)S(1)}, f32[64,512]{1,0:T(8,128)S(1)}, u32[]{:S(2)}, u32[]{:S(2)}) collective-permute-start(f32[64,512]{1,0:T(8,128)S(1)} %add.12), channel_id=1, source_target_pairs={{0,192},{32,224},{64,128},{96,160},{128,64},{160,96},{192,0},{224,... | collective-permute-start | bytes 393224 | tf_op jit(solution)/shard_map/ppermute | solution.py:154
  69.6 0.8 collective-permute-start.2
  70.4 0.0 collective-permute-start.1
  70.4 5.6 %collective-permute-start.17 = (f32[16,512]{1,0:T(8,128)S(1)}, f32[16,512]{1,0:T(8,128)S(1)}, u32[]{:S(2)}, u32[]{:S(2)}) collective-permute-start(f32[16,512]{1,0:T(8,128)S(1)} %reduce_sum.18.refs_0_), channel_id=1, source_target_pairs={{0,28},{1,29},{2,30},{3,31},{4,24},{5,25},{6,26},{7,27},{8,20},{9,... | collective-permute-start | bytes 98312 | tf_op jit(solution)/shard_map/ppermute | solution.py:154
  76.1 0.0 collective-permute-done.3
  76.1 0.0 collective-permute-done.2
  76.1 1.8 %collective-permute-start.9 = (f32[64,512]{1,0:T(8,128)S(1)}, f32[64,512]{1,0:T(8,128)S(1)}, u32[]{:S(2)}, u32[]{:S(2)}) collective-permute-start(f32[64,512]{1,0:T(8,128)S(1)} %add_add_fusion.refs_0_), channel_id=1, source_target_pairs={{0,6},{1,7},{2,4},{3,5},{4,2},{5,3},{6,0},{7,1},{8,14},{9,15},{10,... | collective-permute-start | bytes 393224 | tf_op jit(solution)/shard_map/ppermute | solution.py:154
  78.0 0.0 collective-permute-start.7
  78.0 1.0 collective-permute-start.5
  79.0 5.1 %collective-permute-start.16 = (f32[16,512]{1,0:T(8,128)S(1)}, f32[16,512]{1,0:T(8,128)S(1)}, u32[]{:S(2)}, u32[]{:S(2)}) collective-permute-start(f32[16,512]{1,0:T(8,128)S(1)} %reduce_sum.18.refs_0_), channel_id=1, source_target_pairs={{0,24},{1,25},{2,26},{3,27},{4,28},{5,29},{6,30},{7,31},{8,16},{9,... | collective-permute-start | bytes 98312 | tf_op jit(solution)/shard_map/ppermute | solution.py:154
  84.1 0.0 collective-permute-done.17.refs_7_
  84.1 0.7 collective-permute-start.15
  84.8 1.6 %collective-permute-done.16.refs_6_ = f32[16,512]{1,0:T(8,128)S(1)} collective-permute-done((f32[16,512]{1,0:T(8,128)S(1)}, f32[16,512]{1,0:T(8,128)S(1)}, u32[]{:S(2)}, u32[]{:S(2)}) %collective-permute-start.16) | collective-permute-done | bytes 32800 | tf_op jit(solution)/shard_map/ppermute | solution.py:154
  86.4 3.8 %collective-permute-start.14 = (f32[16,512]{1,0:T(8,128)S(1)}, f32[16,512]{1,0:T(8,128)S(1)}, u32[]{:S(2)}, u32[]{:S(2)}) collective-permute-start(f32[16,512]{1,0:T(8,128)S(1)} %reduce_sum.18.refs_0_), channel_id=1, source_target_pairs={{0,16},{1,17},{2,18},{3,19},{4,20},{5,21},{6,22},{7,23},{8,24},{9,... | collective-permute-start | bytes 98312 | tf_op jit(solution)/shard_map/ppermute | solution.py:154
  90.2 1.7 %collective-permute-start.13 = (f32[16,512]{1,0:T(8,128)S(1)}, f32[16,512]{1,0:T(8,128)S(1)}, u32[]{:S(2)}, u32[]{:S(2)}) collective-permute-start(f32[16,512]{1,0:T(8,128)S(1)} %reduce_sum.18.refs_0_), channel_id=1, source_target_pairs={{0,12},{1,13},{2,14},{3,15},{4,8},{5,9},{6,10},{7,11},{8,4},{9,5},... | collective-permute-start | bytes 98312 | tf_op jit(solution)/shard_map/ppermute | solution.py:154
  91.9 1.2 collective-permute-done.14.refs_4_
  93.1 0.2 collective-permute-start.12
  93.2 1.8 %collective-permute-done.13.refs_3_ = f32[16,512]{1,0:T(8,128)S(1)} collective-permute-done((f32[16,512]{1,0:T(8,128)S(1)}, f32[16,512]{1,0:T(8,128)S(1)}, u32[]{:S(2)}, u32[]{:S(2)}) %collective-permute-start.13) | collective-permute-done | bytes 32800 | tf_op jit(solution)/shard_map/ppermute | solution.py:154
  95.0 0.1 collective-permute-start.11
  95.1 1.9 %collective-permute-done.12.refs_2_ = f32[16,512]{1,0:T(8,128)S(1)} collective-permute-done((f32[16,512]{1,0:T(8,128)S(1)}, f32[16,512]{1,0:T(8,128)S(1)}, u32[]{:S(2)}, u32[]{:S(2)}) %collective-permute-start.12) | collective-permute-done | bytes 32800 | tf_op jit(solution)/shard_map/ppermute | solution.py:154
  97.0 6.9 %collective-permute-start.4 = (f32[64,512]{1,0:T(8,128)S(1)}, f32[64,512]{1,0:T(8,128)S(1)}, u32[]{:S(2)}, u32[]{:S(2)}) collective-permute-start(f32[64,512]{1,0:T(8,128)S(1)} %add_add_fusion.refs_0_), channel_id=1, source_target_pairs={{0,1},{1,0},{2,3},{3,2},{4,5},{5,4},{6,7},{7,6},{8,9},{9,8},{10,11... | collective-permute-start | bytes 393224 | tf_op jit(solution)/shard_map/ppermute | solution.py:154
  103.9 0.0 collective-permute-done.9.refs_6_
  103.9 0.1 collective-permute-start.10
  104.0 1.7 %collective-permute-start.20 = (f32[8,16,512]{2,1,0:T(8,128)S(1)}, f32[8,16,512]{2,1,0:T(8,128)S(1)}, u32[]{:S(2)}, u32[]{:S(2)}) collective-permute-start(f32[8,16,512]{2,1,0:T(8,128)S(1)} %join.1.refs_0_), channel_id=1, source_target_pairs={{0,3},{1,2},{2,1},{3,0},{4,7},{5,6},{6,5},{7,4},{8,11},{9,10},{10,... | collective-permute-start | bytes 786440 | tf_op jit(solution)/shard_map/ppermute | solution.py:154
  105.7 1.2 collective-permute-start.19
  106.9 0.0 collective-permute-done.5.refs_2_
  106.9 0.0 collective-permute-done.4.refs_1_
  106.9 0.5 collective-permute-start.8
  107.4 0.0 collective-permute-done.10.refs_7_
  107.4 0.4 collective-permute-start.6
  107.8 0.8 collective-permute-done.8.refs_5_
  108.6 0.6 copy-done.8
  109.3 23.9 %factor.1.m_hbm = f32[512,512]{1,0:T(8,128)} custom-call(s32[1]{0:T(128)} %bitcast.pos_ref, f32[64,512]{1,0:T(8,128)} %copy-done.2, f32[64,512]{1,0:T(8,128)} %copy-done.6, f32[64,512]{1,0:T(8,128)} %copy-done.5, f32[64,512]{1,0:T(8,128)} %collective-permute-done.6.refs_3_, f32[64,512]{1,0:T(8,128)} %copy-done.4, f32[64,512]{1,0:T(8,128)} %copy-done.8, ...), custom_call_target="tpu_custom_call" | custom-call | tf_op jit(solution)/shard_map/factor/pallas_call | solution.py:190
  133.1 0.0 collective-permute-done.19.refs_2_
  133.2 0.0 collective-permute-done.18.refs_1_
  133.2 0.0 copy-start
  133.2 1.2 copy-done
  134.4 4.1 %update.1 = (f32[512,512]{1,0:T(8,128)}, f32[512,512]{1,0:T(8,128)}) custom-call(s32[1]{0:T(128)} %bitcast.pos_ref, f32[512,512]{1,0:T(8,128)S(1)} %copy-done, f32[512,512]{1,0:T(8,128)S(1)} %copy-done.1, f32[512,512]{1,0:T(8,128)S(1)} %bitcast.2, f32[8,16,512]{2,1,0:T(8,128)S(1)} %join.1.refs_0_, f32[8,16,512]{2,1,0:T(8,128)S(1)} %collective-permute-done.18.refs_1_, ...), custom_call_target="tpu_custom_call" | custom-call | tf_op jit(solution)/shard_map/update/pallas_call | solution.py:212
  (27 shorter events, 0.1 us)
Async XLA Ops:
  12.3 120.9 %copy-start.1 = (f32[512,512]{1,0:T(8,128)S(1)}, f32[512,512]{1,0:T(8,128)}, u32[]{:S(2)}) copy-start(f32[512,512]{1,0:T(8,128)} %trail_hbm.1) | copy-start | bytes 3145732
  27.4 15.1 %all-to-all-start.1 = ((f32[8,48,512]{2,1,0:T(8,128)}), f32[8,48,512]{2,1,0:T(8,128)S(1)}, u32[]{:S(2)}, u32[]{:S(2)}) async-start(f32[8,48,512]{2,1,0:T(8,128)} %get-tuple-element.7), calls=%async_computation.1 | async-start | bytes 1572864 | tf_op jit(solution)/shard_map/all_to_all | solution.py:149
  43.7 89.5 %all-to-all-start.2 = ((f32[8,64,512]{2,1,0:T(8,128)}), f32[8,64,512]{2,1,0:T(8,128)S(1)}, u32[]{:S(2)}, u32[]{:S(2)}) async-start(f32[8,64,512]{2,1,0:T(8,128)} %broadcast_in_dim.2), calls=%async_computation.2 | async-start | bytes 2097152 | tf_op jit(solution)/shard_map/all_to_all | solution.py:149
  48.7 16.5 %collective-permute-start = (f32[64,512]{1,0:T(8,128)}, f32[64,512]{1,0:T(8,128)S(1)}, u32[]{:S(2)}, u32[]{:S(2)}) collective-permute-start(f32[64,512]{1,0:T(8,128)} %get-tuple-element.5), channel_id=1, source_target_pairs={{0,32},{32,0},{64,96},{96,64},{128,160},{160,128},{192,224},{224,1... | collective-permute-start | bytes 393224 | tf_op jit(solution)/shard_map/ppermute | solution.py:154
  66.1 9.9 %collective-permute-start.3 = (f32[64,512]{1,0:T(8,128)S(1)}, f32[64,512]{1,0:T(8,128)S(1)}, u32[]{:S(2)}, u32[]{:S(2)}) collective-permute-start(f32[64,512]{1,0:T(8,128)S(1)} %add.12), channel_id=1, source_target_pairs={{0,192},{32,224},{64,128},{96,160},{128,64},{160,96},{192,0},{224,... | collective-permute-start | bytes 393224 | tf_op jit(solution)/shard_map/ppermute | solution.py:154
  69.6 6.5 %collective-permute-start.2 = (f32[64,512]{1,0:T(8,128)S(1)}, f32[64,512]{1,0:T(8,128)S(1)}, u32[]{:S(2)}, u32[]{:S(2)}) collective-permute-start(f32[64,512]{1,0:T(8,128)S(1)} %add.12), channel_id=1, source_target_pairs={{0,128},{32,160},{64,192},{96,224},{128,0},{160,32},{192,64},{224,... | collective-permute-start | bytes 393224 | tf_op jit(solution)/shard_map/ppermute | solution.py:154
  70.4 5.6 %collective-permute-start.1 = (f32[64,512]{1,0:T(8,128)S(1)}, f32[64,512]{1,0:T(8,128)S(1)}, u32[]{:S(2)}, u32[]{:S(2)}) collective-permute-start(f32[64,512]{1,0:T(8,128)S(1)} %add.12), channel_id=1, source_target_pairs={{0,64},{32,96},{64,0},{96,32},{128,192},{160,224},{192,128},{224,1... | collective-permute-start | bytes 393224 | tf_op jit(solution)/shard_map/ppermute | solution.py:154
  70.4 13.7 %collective-permute-start.17 = (f32[16,512]{1,0:T(8,128)S(1)}, f32[16,512]{1,0:T(8,128)S(1)}, u32[]{:S(2)}, u32[]{:S(2)}) collective-permute-start(f32[16,512]{1,0:T(8,128)S(1)} %reduce_sum.18.refs_0_), channel_id=1, source_target_pairs={{0,28},{1,29},{2,30},{3,31},{4,24},{5,25},{6,26},{7,27},{8,20},{9,... | collective-permute-start | bytes 98312 | tf_op jit(solution)/shard_map/ppermute | solution.py:154
  76.1 33.2 %copy-start.2 = (f32[64,512]{1,0:T(8,128)}, f32[64,512]{1,0:T(8,128)S(1)}, u32[]{:S(2)}) copy-start(f32[64,512]{1,0:T(8,128)S(1)} %add_add_fusion.refs_0_) | copy-start | bytes 393220
  76.1 27.8 %collective-permute-start.9 = (f32[64,512]{1,0:T(8,128)S(1)}, f32[64,512]{1,0:T(8,128)S(1)}, u32[]{:S(2)}, u32[]{:S(2)}) collective-permute-start(f32[64,512]{1,0:T(8,128)S(1)} %add_add_fusion.refs_0_), channel_id=1, source_target_pairs={{0,6},{1,7},{2,4},{3,5},{4,2},{5,3},{6,0},{7,1},{8,14},{9,15},{10,... | collective-permute-start | bytes 393224 | tf_op jit(solution)/shard_map/ppermute | solution.py:154
  78.0 27.7 %collective-permute-start.7 = (f32[64,512]{1,0:T(8,128)S(1)}, f32[64,512]{1,0:T(8,128)S(1)}, u32[]{:S(2)}, u32[]{:S(2)}) collective-permute-start(f32[64,512]{1,0:T(8,128)S(1)} %add_add_fusion.refs_0_), channel_id=1, source_target_pairs={{0,4},{1,5},{2,6},{3,7},{4,0},{5,1},{6,2},{7,3},{8,12},{9,13},{10,... | collective-permute-start | bytes 393224 | tf_op jit(solution)/shard_map/ppermute | solution.py:154
  78.0 28.9 %collective-permute-start.5 = (f32[64,512]{1,0:T(8,128)S(1)}, f32[64,512]{1,0:T(8,128)S(1)}, u32[]{:S(2)}, u32[]{:S(2)}) collective-permute-start(f32[64,512]{1,0:T(8,128)S(1)} %add_add_fusion.refs_0_), channel_id=1, source_target_pairs={{0,2},{1,3},{2,0},{3,1},{4,6},{5,7},{6,4},{7,5},{8,10},{9,11},{10,... | collective-permute-start | bytes 393224 | tf_op jit(solution)/shard_map/ppermute | solution.py:154
  79.0 7.4 %collective-permute-start.16 = (f32[16,512]{1,0:T(8,128)S(1)}, f32[16,512]{1,0:T(8,128)S(1)}, u32[]{:S(2)}, u32[]{:S(2)}) collective-permute-start(f32[16,512]{1,0:T(8,128)S(1)} %reduce_sum.18.refs_0_), channel_id=1, source_target_pairs={{0,24},{1,25},{2,26},{3,27},{4,28},{5,29},{6,30},{7,31},{8,16},{9,... | collective-permute-start | bytes 98312 | tf_op jit(solution)/shard_map/ppermute | solution.py:154
  84.1 6.1 %collective-permute-start.15 = (f32[16,512]{1,0:T(8,128)S(1)}, f32[16,512]{1,0:T(8,128)S(1)}, u32[]{:S(2)}, u32[]{:S(2)}) collective-permute-start(f32[16,512]{1,0:T(8,128)S(1)} %reduce_sum.18.refs_0_), channel_id=1, source_target_pairs={{0,20},{1,21},{2,22},{3,23},{4,16},{5,17},{6,18},{7,19},{8,28},{9,... | collective-permute-start | bytes 98312 | tf_op jit(solution)/shard_map/ppermute | solution.py:154
  86.4 6.7 %collective-permute-start.14 = (f32[16,512]{1,0:T(8,128)S(1)}, f32[16,512]{1,0:T(8,128)S(1)}, u32[]{:S(2)}, u32[]{:S(2)}) collective-permute-start(f32[16,512]{1,0:T(8,128)S(1)} %reduce_sum.18.refs_0_), channel_id=1, source_target_pairs={{0,16},{1,17},{2,18},{3,19},{4,20},{5,21},{6,22},{7,23},{8,24},{9,... | collective-permute-start | bytes 98312 | tf_op jit(solution)/shard_map/ppermute | solution.py:154
  90.2 4.9 %collective-permute-start.13 = (f32[16,512]{1,0:T(8,128)S(1)}, f32[16,512]{1,0:T(8,128)S(1)}, u32[]{:S(2)}, u32[]{:S(2)}) collective-permute-start(f32[16,512]{1,0:T(8,128)S(1)} %reduce_sum.18.refs_0_), channel_id=1, source_target_pairs={{0,12},{1,13},{2,14},{3,15},{4,8},{5,9},{6,10},{7,11},{8,4},{9,5},... | collective-permute-start | bytes 98312 | tf_op jit(solution)/shard_map/ppermute | solution.py:154
  93.1 4.0 %collective-permute-start.12 = (f32[16,512]{1,0:T(8,128)S(1)}, f32[16,512]{1,0:T(8,128)S(1)}, u32[]{:S(2)}, u32[]{:S(2)}) collective-permute-start(f32[16,512]{1,0:T(8,128)S(1)} %reduce_sum.18.refs_0_), channel_id=1, source_target_pairs={{0,8},{1,9},{2,10},{3,11},{4,12},{5,13},{6,14},{7,15},{8,0},{9,1},... | collective-permute-start | bytes 98312 | tf_op jit(solution)/shard_map/ppermute | solution.py:154
  95.0 8.9 %collective-permute-start.11 = (f32[16,512]{1,0:T(8,128)S(1)}, f32[16,512]{1,0:T(8,128)S(1)}, u32[]{:S(2)}, u32[]{:S(2)}) collective-permute-start(f32[16,512]{1,0:T(8,128)S(1)} %reduce_sum.18.refs_0_), channel_id=1, source_target_pairs={{0,4},{1,5},{2,6},{3,7},{4,0},{5,1},{6,2},{7,3},{8,12},{9,13},{10,... | collective-permute-start | bytes 98312 | tf_op jit(solution)/shard_map/ppermute | solution.py:154
  97.0 9.9 %collective-permute-start.4 = (f32[64,512]{1,0:T(8,128)S(1)}, f32[64,512]{1,0:T(8,128)S(1)}, u32[]{:S(2)}, u32[]{:S(2)}) collective-permute-start(f32[64,512]{1,0:T(8,128)S(1)} %add_add_fusion.refs_0_), channel_id=1, source_target_pairs={{0,1},{1,0},{2,3},{3,2},{4,5},{5,4},{6,7},{7,6},{8,9},{9,8},{10,11... | collective-permute-start | bytes 393224 | tf_op jit(solution)/shard_map/ppermute | solution.py:154
  103.9 5.4 %copy-start.3 = (f32[64,512]{1,0:T(8,128)}, f32[64,512]{1,0:T(8,128)S(1)}, u32[]{:S(2)}) copy-start(f32[64,512]{1,0:T(8,128)S(1)} %collective-permute-done.9.refs_6_) | copy-start | bytes 393220
  103.9 3.5 %collective-permute-start.10 = (f32[64,512]{1,0:T(8,128)S(1)}, f32[64,512]{1,0:T(8,128)S(1)}, u32[]{:S(2)}, u32[]{:S(2)}) collective-permute-start(f32[64,512]{1,0:T(8,128)S(1)} %collective-permute-done.9.refs_6_), channel_id=1, source_target_pairs={{0,1},{1,0},{2,3},{3,2},{4,5},{5,4},{6,7},{7,6},{8,9},{9,8},{10,11... | collective-permute-start | bytes 393224 | tf_op jit(solution)/shard_map/ppermute | solution.py:154
  104.0 29.1 %collective-permute-start.20 = (f32[8,16,512]{2,1,0:T(8,128)S(1)}, f32[8,16,512]{2,1,0:T(8,128)S(1)}, u32[]{:S(2)}, u32[]{:S(2)}) collective-permute-start(f32[8,16,512]{2,1,0:T(8,128)S(1)} %join.1.refs_0_), channel_id=1, source_target_pairs={{0,3},{1,2},{2,1},{3,0},{4,7},{5,6},{6,5},{7,4},{8,11},{9,10},{10,... | collective-permute-start | bytes 786440 | tf_op jit(solution)/shard_map/ppermute | solution.py:154
  105.7 1.7 %copy-start.4 = (f32[64,512]{1,0:T(8,128)}, f32[64,512]{1,0:T(8,128)S(1)}, u32[]{:S(2)}) copy-start(f32[64,512]{1,0:T(8,128)S(1)} %collective-permute-done.7.refs_4_) | copy-start | bytes 393220
  105.7 27.4 %collective-permute-start.19 = (f32[8,16,512]{2,1,0:T(8,128)S(1)}, f32[8,16,512]{2,1,0:T(8,128)S(1)}, u32[]{:S(2)}, u32[]{:S(2)}) collective-permute-start(f32[8,16,512]{2,1,0:T(8,128)S(1)} %join.1.refs_0_), channel_id=1, source_target_pairs={{0,2},{1,3},{2,0},{3,1},{4,6},{5,7},{6,4},{7,5},{8,10},{9,11},{10,... | collective-permute-start | bytes 786440 | tf_op jit(solution)/shard_map/ppermute | solution.py:154
  106.9 1.7 %copy-start.5 = (f32[64,512]{1,0:T(8,128)}, f32[64,512]{1,0:T(8,128)S(1)}, u32[]{:S(2)}) copy-start(f32[64,512]{1,0:T(8,128)S(1)} %collective-permute-done.5.refs_2_) | copy-start | bytes 393220
  106.9 26.3 %collective-permute-start.18 = (f32[8,16,512]{2,1,0:T(8,128)S(1)}, f32[8,16,512]{2,1,0:T(8,128)S(1)}, u32[]{:S(2)}, u32[]{:S(2)}) collective-permute-start(f32[8,16,512]{2,1,0:T(8,128)S(1)} %join.1.refs_0_), channel_id=1, source_target_pairs={{0,1},{1,0},{2,3},{3,2},{4,5},{5,4},{6,7},{7,6},{8,9},{9,8},{10,11... | collective-permute-start | bytes 786440 | tf_op jit(solution)/shard_map/ppermute | solution.py:154
  106.9 1.7 %copy-start.6 = (f32[64,512]{1,0:T(8,128)}, f32[64,512]{1,0:T(8,128)S(1)}, u32[]{:S(2)}) copy-start(f32[64,512]{1,0:T(8,128)S(1)} %collective-permute-done.4.refs_1_) | copy-start | bytes 393220
  106.9 1.7 %collective-permute-start.8 = (f32[64,512]{1,0:T(8,128)S(1)}, f32[64,512]{1,0:T(8,128)S(1)}, u32[]{:S(2)}, u32[]{:S(2)}) collective-permute-start(f32[64,512]{1,0:T(8,128)S(1)} %collective-permute-done.7.refs_4_), channel_id=1, source_target_pairs={{0,1},{1,0},{2,3},{3,2},{4,5},{5,4},{6,7},{7,6},{8,9},{9,8},{10,11... | collective-permute-start | bytes 393224 | tf_op jit(solution)/shard_map/ppermute | solution.py:154
  107.4 1.2 copy-start.7
  107.4 1.9 %collective-permute-start.6 = (f32[64,512]{1,0:T(8,128)S(1)}, f32[64,512]{1,0:T(8,128)}, u32[]{:S(2)}, u32[]{:S(2)}) collective-permute-start(f32[64,512]{1,0:T(8,128)S(1)} %collective-permute-done.5.refs_2_), channel_id=1, source_target_pairs={{0,1},{1,0},{2,3},{3,2},{4,5},{5,4},{6,7},{7,6},{8,9},{9,8},{10,11... | collective-permute-start | bytes 393224 | tf_op jit(solution)/shard_map/ppermute | solution.py:154
  108.6 0.6 copy-start.8
  133.2 1.2 copy-start
